TPU v7x, 32 devices: a whole 2x2x4 slice. The times are simulated.
32 devices in a mesh: dp: 16 (over z, y, core), tensor: 2 (over x).
Axes of the slice: x: 2, y: 2, z: 4, core: 2. Of those that a mesh axis runs over, the one named last changes fastest.
Arguments:
- x_in: bfloat16 [32768, 768], P(('dp', 'tensor')), may hold values from -6 to 6
- lengths: int32 [32], P('dp'), may hold values from 256 to 1024, as said below
- cotangent: bfloat16 [32768, 768], P(('dp', 'tensor')), may hold values from -6 to 6
- w_query: bfloat16 [768, 768], P('dp', 'tensor'), may hold values from -0.5 to 0.5
- w_key: bfloat16 [768, 768], P('dp', 'tensor'), may hold values from -0.5 to 0.5
- w_value: bfloat16 [768, 768], P('dp', 'tensor'), may hold values from -0.21875 to 0.21875
- w_out: bfloat16 [768, 768], P('tensor', 'dp'), may hold values from -0.21875 to 0.21875
- w_in: bfloat16 [768, 3072], P('dp', 'tensor'), may hold values from -0.21875 to 0.21875
- w_down: bfloat16 [3072, 768], P('tensor', 'dp'), may hold values from -0.109375 to 0.109375
- conv_weight: float32 [12, 33], P('tensor'), may hold values from -1 to 1
- ln1_gain: float32 [768], P(('dp', 'tensor')), may hold values from 0.5 to 1.5
- ln1_bias: float32 [768], P(('dp', 'tensor')), may hold values from -1.8 to 1.8
- ln2_gain: float32 [768], P(('dp', 'tensor')), may hold values from 0.5 to 1.5
- ln2_bias: float32 [768], P(('dp', 'tensor')), may hold values from -1.8 to 1.8
Outputs:
- output: bfloat16 [32768, 768], P(('dp', 'tensor'))
- input_grad: bfloat16 [32768, 768], P(('dp', 'tensor'))
- grad_query: float32 [768, 768], P('dp', 'tensor')
- grad_key: float32 [768, 768], P('dp', 'tensor')
- grad_value: float32 [768, 768], P('dp', 'tensor')
- grad_out: float32 [768, 768], P('tensor', 'dp')
- grad_in: float32 [768, 3072], P('dp', 'tensor')
- grad_down: float32 [3072, 768], P('tensor', 'dp')
- grad_conv: float32 [12, 33], P('tensor')
- grad_ln1_gain: float32 [768], P(('dp', 'tensor'))
- grad_ln1_bias: float32 [768], P(('dp', 'tensor'))
- grad_ln2_gain: float32 [768], P(('dp', 'tensor'))
- grad_ln2_bias: float32 [768], P(('dp', 'tensor'))
- stats: float32 [3], replicated
Inputs may be any that keep to these rules, and one draw needn't show every extreme that they name: `lengths`: the valid tokens of a sequence are its first ones; in every draw some sequence fills all 1024 slots.
All inputs are finite; a program needn't handle non-finite values.
Results may differ from a plain program's by a relative error of at most 0.017.
Values may be sent and summed in bfloat16 or wider, within the bound.
A program may use at most 320 MiB of HBM per device.

v0:
```python
from functools import partial

import jax
import jax.numpy as jnp
from jax import lax
from jax.experimental import pallas as pl
from jax.experimental.pallas import tpu as pltpu
from jax.sharding import PartitionSpec as P

ANY = pl.BlockSpec(memory_space=pl.ANY)
F32, BF = jnp.float32, jnp.bfloat16
NN, NT, TN = ((1,), (0,)), ((1,), (1,)), ((0,), (0,))
MARKS = 64
HEAD = 64
PACK = 4
WIDE = PACK * HEAD
TAPS = 33
EDGE = TAPS // 2
ROWS = 128
TALL = 256
TAPS_AT, FLIP_AT, BLOCK = 8, 16, 24
STATS = 36
WINDOW = ROWS + 2 * EDGE
STEPS = 6
KEPT = 4


def mm(a, b, dims=NN):
    return lax.dot_general(a, b, (dims, ((), ())), preferred_element_type=F32)


def halves(a):
    high = a.astype(BF)
    return high, (a - high.astype(F32)).astype(BF)


def mm3(a, b, dims=NN):
    (ah, al), (bh, bl) = a, b
    return mm(ah, bh, dims) + (mm(ah, bl, dims) + mm(al, bh, dims))


def mm3f(a, b, dims=NN):
    return mm3(halves(a), halves(b), dims)


def grid_of(shape):
    return (
        lax.broadcasted_iota(jnp.int32, shape, 0),
        lax.broadcasted_iota(jnp.int32, shape, 1),
    )


def block_mask():
    row, col = grid_of((WIDE, WIDE))
    return row // HEAD == col // HEAD


def eye():
    row, col = grid_of((WIDE, WIDE))
    return (row == col).astype(F32)


def spread(packed, mask):
    full = jnp.concatenate([packed] * PACK, axis=0)
    return jnp.where(mask, full, jnp.zeros_like(full))


def gather_up(full):
    return sum(full[i * MARKS : (i + 1) * MARKS] for i in range(PACK))


def segment_reduce(a, fill, op):
    lane = lax.broadcasted_iota(jnp.int32, (a.shape[0], 128), 1) < HEAD
    parts = []
    for tile in range(a.shape[1] // 128):
        piece = a[:, tile * 128 : (tile + 1) * 128]
        low = op(jnp.where(lane, piece, fill), axis=1, keepdims=True)
        high = op(jnp.where(lane, fill, piece), axis=1, keepdims=True)
        parts.append(jnp.where(lane, low, high))
    return jnp.concatenate(parts, axis=1)


def average_matrix():
    row, col = grid_of((TALL // 16, TALL))
    return jnp.where(row == col // 16, 1.0 / 16, 0.0).astype(BF)


def average_back():
    row, col = grid_of((ROWS, ROWS // 16))
    return jnp.where(row // 16 == col, 1.0 / 16, 0.0).astype(BF)


def lanes_of(group):
    return slice(group * WIDE, (group + 1) * WIDE)


def put(ref, rows, which, wide, parts, start, value):
    share = wide // parts
    for tile in range(0, value.shape[1], 128):
        lane = start + tile
        at = (3 * (lane // share) + which) * share + lane % share
        ref[rows, at : at + 128] = value[:, tile : tile + 128]


def lhs(a):
    return jnp.concatenate(halves(a), axis=1)


def rhs(b):
    high, low = halves(b)
    return jnp.concatenate(
        [
            jnp.concatenate([high, low], axis=1),
            jnp.concatenate([high, jnp.zeros_like(high)], axis=1),
        ],
        axis=0,
    )


def pair_mm(left, right):
    out = mm(left, right)
    return out[:, :128] + out[:, 128:]


def fold(full):
    return full[:MARKS] + full[MARKS:]


def unfold(packed, mask):
    full = jnp.concatenate([packed, packed], axis=0)
    return jnp.where(mask, full, 0.0)


def pair_lanes(pair):
    return slice(pair * 128, (pair + 1) * 128)


def pair_consts():
    row, col = grid_of((128, 128))
    return row // HEAD == col // HEAD, (row == col).astype(F32)


def toeplitz(taps_ref, first, own_heads, group):
    parts = []
    for i in range(PACK):
        half, head = divmod(group * PACK + i, own_heads)
        line = taps_ref[first + head : first + head + 1, half * 128 : (half + 1) * 128]
        line = jnp.concatenate([line, jnp.zeros_like(line)], axis=1)
        line = jnp.broadcast_to(line, (ROWS, 256))
        parts.append(pltpu.roll(line, 0, 1, stride=1, stride_axis=0)[:, :WINDOW])
    return jnp.concatenate(parts, axis=0).astype(BF)


def diagonal_lanes(stacked):
    col = lax.broadcasted_iota(jnp.int32, (ROWS, WIDE), 1) // HEAD
    out = stacked[:ROWS]
    for i in range(1, PACK):
        out = jnp.where(col == i, stacked[i * ROWS : (i + 1) * ROWS], out)
    return out


def attn_fwd_kernel(slot, groups, parts, own, *refs):
    len_ref, x_ref = refs[:2]
    if own:
        shards, outs, refs = refs[2:9], refs[9:14], refs[14:]
        weight, taps_ref = outs[0], outs[1].at[0, 0, 0, 0]
    else:
        weight, taps_ref, refs = refs[2], refs[3], refs[4:]
    ctx_ref, qh_ref, kh_ref, vp_ref, k1_ref, k3_ref, small_ref, chain_ref = refs[:8]
    z_ref, k2_ref, s_ref, top_ref, t_ref = refs[8:13]
    moves = []
    if own:
        place = Place()
        greet(place)
        moves = gather_parts(place, GATHERS, shards, outs, *refs[13:])

    def advance(name):
        for which, stage in GATHER_AT.get(name, ()) if own else ():
            for part, wave in zip(moves, GATHER_WAVES):
                if wave == which:
                    part.run(stage)

    advance("start")
    count = slot // ROWS
    scale = HEAD ** -0.25
    length = len_ref[lax.axis_index("tensor")] if len_ref.shape[0] > 1 else len_ref[0]
    avg = average_matrix()
    wide = groups * WIDE
    share = wide // parts
    own_heads = share // HEAD
    vp_ref[0:EDGE, :] = jnp.zeros((EDGE, wide), BF)
    vp_ref[slot + EDGE : slot + 2 * EDGE, :] = jnp.zeros((EDGE, wide), BF)

    def columns(start, width):
        if own:
            return weight[:, :, :, :, :, start : start + width].reshape(-1, width)
        return weight[:, start : start + width]

    def valid_of(i, rows):
        row = lax.broadcasted_iota(jnp.int32, (rows, 1), 0) + i * rows
        return (row < length).astype(F32)

    def load(i, carry):
        rows = pl.ds(pl.multiple_of(i * TALL, TALL), TALL)
        few = pl.ds(pl.multiple_of(i * (TALL // 16), TALL // 16), TALL // 16)
        factor = valid_of(i, TALL) * scale
        for p in range(parts):
            both = mm(x_ref[rows, :], columns(3 * p * share, 2 * share)) * factor
            at = slice(p * share, (p + 1) * share)
            high, low = halves(both)
            qh_ref[rows, at] = high[:, :share]
            kh_ref[rows, at] = high[:, share:]
            means = mm(avg, high) + mm(avg, low)
            small_ref[0, few, at] = means[:, :share]
            small_ref[1, few, at] = means[:, share:]
        return carry

    lax.fori_loop(0, slot // TALL, load, 0)
    advance("load")
    mask = block_mask()
    pmask, one = pair_consts()
    pairs = 2 * groups

    for j in range(pairs):
        at = pair_lanes(j)
        ql, kl = unfold(small_ref[0, :, at], pmask), unfold(small_ref[1, :, at], pmask)
        a2 = jnp.where(pmask, mm3f(ql, kl, NT), -1e30)
        e2 = jnp.where(pmask, jnp.exp(a2 - jnp.max(a2, axis=1, keepdims=True)), 0.0)
        k2 = e2 / jnp.sum(e2, axis=1, keepdims=True)
        top = segment_reduce(jnp.sum(k2, axis=0, keepdims=True), -1e30, jnp.max)
        k2_ref[j] = lhs(k2)
        small_ref[2, :, at] = fold(k2)
        z_ref[j] = jnp.transpose(k2) / top

    def newton(step, carry):
        every = range(pairs)
        z = [z_ref[j] for j in every]
        p = [pair_mm(k2_ref[j], rhs(z[j])) for j in every]
        left = [lhs(p[j]) for j in every]
        t2 = [15.0 * one - pair_mm(left[j], rhs(7.0 * one - p[j])) for j in every]
        t3 = [13.0 * one - pair_mm(left[j], rhs(t2[j])) for j in every]
        new = [0.25 * pair_mm(lhs(z[j]), rhs(t3[j])) for j in every]
        for j in every:
            for n, value in enumerate((z, p, t2, t3)):
                chain_ref[step, n, :, pair_lanes(j)] = fold(value[j])
            z_ref[j] = new[j]
        return carry

    lax.fori_loop(0, STEPS // 2, newton, 0)
    advance("newton0")
    lax.fori_loop(STEPS // 2, STEPS, newton, 0)
    advance("newton1")

    for g in range(groups):
        at = lanes_of(g)
        ql = spread(small_ref[0, :, at], mask).astype(BF)
        top_ref[...] = jnp.full(top_ref.shape, -jnp.inf, F32)

        def scores(i, carry):
            rows = pl.ds(pl.multiple_of(i * ROWS, ROWS), ROWS)
            row = lax.broadcasted_iota(jnp.int32, (ROWS, 1), 0) + i * ROWS
            a3 = jnp.where(row < length, mm(kh_ref[rows, at], ql, NT), -1e9)
            s_ref[rows, :] = a3
            top_ref[0:1, :] = jnp.maximum(top_ref[0:1, :], jnp.max(a3, axis=0, keepdims=True))
            return carry

        lax.fori_loop(0, count, scores, 0)
        peak = top_ref[0:1, :]
        top_ref[0:1, :] = jnp.zeros((1, WIDE), F32)

        def powers(i, carry):
            rows = pl.ds(pl.multiple_of(i * ROWS, ROWS), ROWS)
            e3 = jnp.exp(s_ref[rows, :] - peak)
            s_ref[rows, :] = e3
            top_ref[0:1, :] += jnp.sum(e3, axis=0, keepdims=True)
            return carry

        lax.fori_loop(0, count, powers, 0)
        inverse = 1.0 / top_ref[0:1, :]

        def weigh(i, carry):
            rows = pl.ds(pl.multiple_of(i * ROWS, ROWS), ROWS)
            k3_ref[rows, at] = (s_ref[rows, :] * inverse).astype(BF)
            return carry

        lax.fori_loop(0, count, weigh, 0)
        advance(f"third{g}")

    ones = mask.astype(F32).astype(BF)
    for g in range(groups):
        at = lanes_of(g)
        kl = spread(small_ref[1, :, at], mask).astype(BF)

        def first(i, carry):
            rows = pl.ds(pl.multiple_of(i * ROWS, ROWS), ROWS)
            a1 = mm(qh_ref[rows, at], kl, NT)
            e1 = jnp.exp(a1 - segment_reduce(a1, -jnp.inf, jnp.max)).astype(BF)
            k1_ref[rows, at] = (e1.astype(F32) / mm(e1, ones)).astype(BF)
            return carry

        lax.fori_loop(0, count, first, 0)
        advance(f"first{g}")

    def load_values(i, carry):
        rows = pl.ds(pl.multiple_of(i * TALL + EDGE, EDGE), TALL)
        valid = valid_of(i, TALL)
        x = x_ref[pl.ds(pl.multiple_of(i * TALL, TALL), TALL), :]
        for p in range(parts):
            value = mm(x, columns((3 * p + 2) * share, share)) * valid
            vp_ref[rows, p * share : (p + 1) * share] = value.astype(BF)
        return carry

    lax.fori_loop(0, slot // TALL, load_values, 0)

    for g in range(groups):
        at = lanes_of(g)
        b = mm(k3_ref[:, at], vp_ref[EDGE : slot + EDGE, at], TN)
        b = jnp.where(mask, b, 0.0)
        for sub in range(2):
            j, inner = 2 * g + sub, pair_lanes(sub)
            z, piece = z_ref[j], b[inner, inner]
            small_ref[3, :, pair_lanes(j)] = fold(piece)
            small_ref[4, :, pair_lanes(j)] = fold(mm3f(z, piece))
            small_ref[5, :, pair_lanes(j)] = fold(z)
        t_ref[...] = toeplitz(taps_ref, TAPS_AT, own_heads, g)
        cb = spread(small_ref[4, :, at], mask).astype(BF)

        def mix(i, carry):
            rows = pl.ds(pl.multiple_of(i * ROWS, ROWS), ROWS)
            window = vp_ref[pl.ds(pl.multiple_of(i * ROWS, ROWS), WINDOW), at]
            ctx_ref[rows, at] = (
                mm(k1_ref[rows, at], cb) + diagonal_lanes(mm(t_ref[...], window))
            ).astype(BF)
            return carry

        lax.fori_loop(0, count, mix, 0)
        advance(f"mix{g}")
    advance("end")


def attn_bwd_kernel(slot, groups, parts, own, *refs):
    (len_ref, g_ref, qh_ref, kh_ref, vp_ref, k1_ref, k3_ref, small_ref, chain_ref, taps_ref,
     xt_ref, w_ref, dres_ref, block_ref) = refs[:14]
    if own:
        fulls, quarter_ref, refs = refs[14:16], refs[16], refs[17:]
        outs, down_out, refs = refs[:5], refs[5], refs[6:]
    else:
        outs, refs = (refs[14],), refs[15:]
    late_ref = {}
    for n, (name, ref) in enumerate(
        (("chain", chain_ref), ("xt", xt_ref), ("w", w_ref), ("dres", dres_ref))
    ):
        late_ref[name] = pltpu.make_async_copy(ref, refs[2 + n], refs[6].at[n])
    chain_ref, xt_ref, w_ref, dres_ref = refs[2:6]
    dx_ref, sum_ref = refs[:2]
    refs = refs[:2] + refs[7:]
    (dqkv_ref, gp_ref, da1_ref, da3_ref, dk_ref, dz_ref, k2_ref,
     dql_ref, dkl_ref, t_ref, acc_ref) = refs[2:13]
    todo = {}
    wide_of = groups * WIDE
    if own:
        grad_ref, totals, landed = refs[13:16]
        place = Place()
        greet(place)
        scatters = scatter_parts(place, SCATTERS, fulls + (grad_ref,), outs, refs[19:])
        base = SUM_COPIES * len(SCATTERS)
        total = Total(place, totals.at[0], sum_ref, totals, landed, refs[-3], refs[-2], base, wide_of)
        tail = ScatterEnd(place, quarter_ref, down_out, refs[16:19], refs[-3], refs[-2], base + 5)
        todo = SCATTER_AT
    else:
        grad_ref = outs[0]
        totals = sum_ref

    def advance(name):
        for which, stage in todo.get(name, ()):
            if which == "t":
                total.run(stage)
            elif which == "d":
                tail.run(stage)
            else:
                for part, wave in zip(scatters, SCATTER_WAVES):
                    if wave == which:
                        part.run(stage)

    advance("start")
    for copy in late_ref.values():
        copy.start()
    count = slot // ROWS
    marks = ROWS // 16
    scale = HEAD ** -0.25
    length = len_ref[lax.axis_index("tensor")] if len_ref.shape[0] > 1 else len_ref[0]
    wide = groups * WIDE
    share = wide // parts
    own_heads = share // HEAD
    pairs = 2 * groups
    mask = block_mask()
    pmask, one = pair_consts()
    ones = mask.astype(F32).astype(BF)
    gp_ref[0:EDGE, :] = jnp.zeros((EDGE, wide), BF)
    gp_ref[slot + EDGE : slot + 2 * EDGE, :] = jnp.zeros((EDGE, wide), BF)
    gp_ref[EDGE : slot + EDGE, :] = g_ref[...]
    col = lax.broadcasted_iota(jnp.int32, (ROWS, WIDE), 1) // HEAD
    up, across = grid_of((ROWS, ROWS))
    flip = jnp.where(up + across == ROWS - 1, 1.0, 0.0).astype(BF)
    taps_lane = lax.broadcasted_iota(jnp.int32, (1, 128), 1) < TAPS

    def totals_row(row):
        return (0, slice(row, row + 1)) if own else slice(row, row + 1)

    if own:
        totals[0] = block_ref[...]
    else:
        sum_ref[...] = block_ref[...]

    for g in range(groups):
        at = lanes_of(g)
        cb = spread(small_ref[4, :, at], mask).astype(BF)

        def first(i, carry):
            rows = pl.ds(pl.multiple_of(i * ROWS, ROWS), ROWS)
            k1 = k1_ref[rows, at].astype(F32)
            dk1 = mm(g_ref[rows, at], cb, NT)
            high, low = halves(dk1 * k1)
            da1_ref[rows, at] = (k1 * (dk1 - (mm(high, ones) + mm(low, ones)))).astype(BF)
            return carry

        lax.fori_loop(0, count, first, 0)
        advance(f"first{g}")
        dc = jnp.where(mask, mm(k1_ref[:, at], g_ref[:, at], TN), 0.0)
        dkl_ref[:, at] = gather_up(jnp.where(mask, mm(da1_ref[:, at], qh_ref[:, at], TN), 0.0))
        many = jnp.ones((8, 128), BF)
        totals_of = []
        for sub in range(2):
            j, inner = 2 * g + sub, pair_lanes(sub)
            b, z = (unfold(small_ref[n, :, pair_lanes(j)], pmask) for n in (3, 5))
            piece = halves(dc[inner, inner])
            dz_ref[j] = mm3(halves(b), piece, NT)
            db = mm3(halves(z), piece, TN)
            dql_ref[:, pair_lanes(j)] = fold(db)
            high, low = halves(db * b)
            totals_of.append((mm(many, high, NT) + mm(many, low, NT))[0:1, :])
        peak = jnp.concatenate(totals_of, axis=1)
        dbb = spread(dql_ref[:, at], mask).astype(BF)
        t_ref[...] = toeplitz(taps_ref, FLIP_AT, own_heads, g)
        acc_ref[...] = jnp.zeros(acc_ref.shape, F32)

        def second(i, carry):
            rows = pl.ds(pl.multiple_of(i * ROWS, ROWS), ROWS)
            row = lax.broadcasted_iota(jnp.int32, (ROWS, 1), 0) + i * ROWS
            valid = (row < length).astype(F32)
            k3 = k3_ref[rows, at]
            vh = vp_ref[pl.ds(pl.multiple_of(i * ROWS + EDGE, EDGE), ROWS), at]
            dk3 = mm(vh, dbb, NT)
            da3_ref[rows, at] = (k3.astype(F32) * (dk3 - peak)).astype(BF)
            window = pl.ds(pl.multiple_of(i * ROWS, ROWS), WINDOW)
            dv = mm(k3, dbb) + diagonal_lanes(mm(t_ref[...], gp_ref[window, at]))
            put(dqkv_ref, rows, 2, wide, parts, g * WIDE, (dv * valid).astype(BF))
            grad = g_ref[rows, at]
            split = jnp.concatenate(
                [jnp.where(col == h, grad, jnp.zeros_like(grad)) for h in range(PACK)], axis=0
            )
            acc_ref[:, :WINDOW] += mm(split, vp_ref[window, at], NT)
            return carry

        lax.fori_loop(0, count, second, 0)
        for h in range(PACK):
            high, low = halves(acc_ref[h * ROWS : (h + 1) * ROWS, :])
            turned = pltpu.roll(mm(flip, high) + mm(flip, low), 0, 1, stride=1, stride_axis=0)
            line = pltpu.roll(jnp.sum(turned, axis=0, keepdims=True), 129, 1)[:, :128]
            totals[totals_row(24 + g * PACK + h)] = jnp.where(taps_lane, line, 0.0)
        dql_ref[:, at] = gather_up(jnp.where(mask, mm(da3_ref[:, at], kh_ref[:, at], TN), 0.0))
        advance(f"second{g}")

    def weight_grad(start, width):
        size = xt_ref.shape[0] // 4

        def block_grad(block, carry):
            rows = pl.ds(pl.multiple_of(block * size, 64), size)
            for p in range(parts):
                lanes = slice(3 * p * share + start, 3 * p * share + start + width)
                here = mm(xt_ref[rows, :], dqkv_ref[:, lanes]).astype(BF)
                if own:
                    four = here.reshape(2, 2, grad_ref.shape[-2], width)
                    grad_ref[block // 2, block % 2, :, :, :, lanes] = four
                else:
                    grad_ref[rows, lanes] = here
            return carry

        lax.fori_loop(0, 4, block_grad, 0)

    late_ref["xt"].wait()
    weight_grad(2 * share, share)
    advance("values")
    late_ref["chain"].wait()
    for j in range(pairs):
        dk_ref[j] = jnp.zeros((128, 128), F32)
        k2_ref[j] = unfold(small_ref[2, :, pair_lanes(j)], pmask)

    def newton(back, carry):
        step = STEPS - 1 - back
        every = range(pairs)
        z, p, t2, t3 = (
            [unfold(chain_ref[step, n, :, pair_lanes(j)], pmask) for j in every] for n in range(KEPT)
        )
        dz = [0.25 * dz_ref[j] for j in every]
        dt3 = [pair_mm(lhs(dz[j]), rhs(z[j])) for j in every]
        dt2 = [-pair_mm(lhs(dt3[j]), rhs(p[j])) for j in every]
        dp = [pair_mm(lhs(dt2[j]), rhs(p[j])) - pair_mm(lhs(t2[j]), rhs(dt3[j])) for j in every]
        dp = [dp[j] - pair_mm(lhs(7.0 * one - p[j]), rhs(dt2[j])) for j in every]
        for j in every:
            dk_ref[j] += pair_mm(lhs(z[j]), rhs(dp[j]))
        new = [pair_mm(lhs(t3[j]), rhs(dz[j])) + pair_mm(lhs(dp[j]), rhs(k2_ref[j])) for j in every]
        for j in every:
            dz_ref[j] = new[j]
        return carry

    for third_of in range(3):
        lax.fori_loop(third_of * STEPS // 3, (third_of + 1) * STEPS // 3, newton, 0)
        advance(f"newton{third_of}")

    for j in range(pairs):
        at = pair_lanes(j)
        k2 = k2_ref[j]
        sums = jnp.sum(k2, axis=0, keepdims=True)
        top = segment_reduce(sums, -1e30, jnp.max)
        hit = (sums == top).astype(F32)
        ties = segment_reduce(hit, 0.0, jnp.sum)
        dz0 = dz_ref[j]
        dtop = -segment_reduce(jnp.sum(dz0 * k2, axis=0, keepdims=True), 0.0, jnp.sum) / (top * top)
        dk2 = jnp.where(pmask, jnp.transpose(dk_ref[j]) + dz0 / top + hit * (dtop / ties), 0.0)
        da2 = halves(k2 * (dk2 - jnp.sum(dk2 * k2, axis=1, keepdims=True)))
        qls, kls = (halves(unfold(small_ref[n, :, at], pmask)) for n in (0, 1))
        dql_ref[:, at] += fold(mm3(da2, kls))
        dkl_ref[:, at] += fold(mm3(da2, qls, TN))
    back = average_back()

    for g in range(groups):
        at = lanes_of(g)
        qlb, klb = (spread(small_ref[n, :, at].astype(BF), mask) for n in (0, 1))

        def third(i, carry):
            rows = pl.ds(pl.multiple_of(i * ROWS, ROWS), ROWS)
            few = pl.ds(pl.multiple_of(i * marks, marks), marks)
            row = lax.broadcasted_iota(jnp.int32, (ROWS, 1), 0) + i * ROWS
            valid = jnp.where(row < length, scale, 0.0)
            dq = mm(da1_ref[rows, at], klb) + mm(back, dql_ref[few, at].astype(BF))
            dk = mm(da3_ref[rows, at], qlb) + mm(back, dkl_ref[few, at].astype(BF))
            put(dqkv_ref, rows, 0, wide, parts, g * WIDE, (dq * valid).astype(BF))
            put(dqkv_ref, rows, 1, wide, parts, g * WIDE, (dk * valid).astype(BF))
            return carry

        lax.fori_loop(0, count, third, 0)
        advance(f"third{g}")

    weight_grad(0, share)
    advance("queries")
    weight_grad(share, share)
    advance("keys")
    late_ref["w"].wait()
    late_ref["dres"].wait()

    def input_rows(i, carry):
        rows = pl.ds(pl.multiple_of(i * TALL, TALL), TALL)
        dx_ref[rows, :] = (dres_ref[rows, :] + mm(dqkv_ref[rows, :], w_ref[...], NT)).astype(BF)
        return carry

    for half in range(2):
        turns = slot // TALL // 2
        lax.fori_loop(half * turns, (half + 1) * turns, input_rows, 0)
        advance(f"input{half}")
    advance("end")


VM = pl.BlockSpec(memory_space=pltpu.VMEM)
SM = pl.BlockSpec(memory_space=pltpu.SMEM)
LIMIT = 60 * 1024 * 1024


def attn_fwd(length, x, parts, own, weights):
    slot, wide = x.shape
    groups = wide // WIDE
    shape = jax.ShapeDtypeStruct
    talks = dict(collective_id=1, has_side_effects=True) if own else {}
    gathered = gather_shapes(weights[0].shape[0], wide, 2 * weights[-1].shape[1]) if own else ()
    outs = pl.pallas_call(
        partial(attn_fwd_kernel, slot, groups, parts, own),
        out_shape=gathered
        + (
            shape((slot, wide), BF),
            shape((slot, wide), BF),
            shape((slot, wide), BF),
            shape((slot + 2 * EDGE, wide), BF),
            shape((slot, wide), BF),
            shape((slot, wide), BF),
            shape((6, MARKS, wide), F32),
            shape((STEPS, KEPT, MARKS, wide), F32),
        ),
        in_specs=[SM, VM] + [VM] * len(weights),
        out_specs=([VM, VM, ANY, ANY, ANY] if own else []) + [VM] * 8,
        scratch_shapes=[
            pltpu.VMEM((2 * groups, 128, 128), F32),
            pltpu.VMEM((2 * groups, 128, 256), BF),
            pltpu.VMEM((slot, WIDE), F32),
            pltpu.VMEM((8, WIDE), F32),
            pltpu.VMEM((PACK * ROWS, WINDOW), BF),
        ]
        + (gather_scratch(GATHERS) if own else []),
        compiler_params=pltpu.CompilerParams(vmem_limit_bytes=LIMIT, **talks),
        name="attn_fwd",
    )(length, x, *weights)
    return outs[: len(gathered)], outs[len(gathered) :]


def attn_bwd(length, g, saved, taps, xt, weight, dres, block, parts, own, fulls, quarter=None):
    slot, wide = g.shape
    groups = wide // WIDE
    shape = jax.ShapeDtypeStruct
    talks = dict(collective_id=2, has_side_effects=True) if own else {}
    ends = (shape((slot, wide), BF), shape(block.shape, F32))
    if own:
        rows = fulls[0].shape[0] // 16
        fulls = [f.reshape(2, 2, 2, 2, rows, f.shape[1]) for f in fulls]
        width = quarter.shape[-1]
        outs = (shape((rows, wide // 2), F32), shape((rows, width), F32))
        outs += (shape((rows, wide // 2), F32),) * 3 + (shape((rows, width), F32),)
        extra = [
            pltpu.VMEM((2, 2, 2, 2, rows, 3 * wide), BF),
            pltpu.VMEM((6,) + block.shape, F32),
            pltpu.VMEM((5,) + block.shape, F32),
            pltpu.VMEM((2, rows, width), BF),
            pltpu.VMEM((2, rows, width), BF),
            pltpu.VMEM((rows, width), BF),
        ] + all_scatter_scratch(SCATTERS, rows, 7)
    else:
        fulls, extra = [], []
        outs = (shape((wide, 3 * wide), BF),)
    return pl.pallas_call(
        partial(attn_bwd_kernel, slot, groups, parts, own),
        out_shape=outs + ends,
        in_specs=[SM] + [VM] * 7 + [ANY, VM, ANY, ANY, ANY, VM] + [ANY] * len(fulls) + ([VM] if own else []),
        out_specs=[VM] * (len(outs) + 2),
        scratch_shapes=[
            pltpu.VMEM(saved[-1].shape, F32),
            pltpu.VMEM(xt.shape, BF),
            pltpu.VMEM(weight.shape, BF),
            pltpu.VMEM(dres.shape, F32),
            pltpu.SemaphoreType.DMA((4,)),
            pltpu.VMEM((slot, 3 * wide), BF),
            pltpu.VMEM((slot + 2 * EDGE, wide), BF),
            pltpu.VMEM((slot, wide), BF),
            pltpu.VMEM((slot, wide), BF),
            pltpu.VMEM((2 * groups, 128, 128), F32),
            pltpu.VMEM((2 * groups, 128, 128), F32),
            pltpu.VMEM((2 * groups, 128, 128), F32),
            pltpu.VMEM((MARKS, wide), F32),
            pltpu.VMEM((MARKS, wide), F32),
            pltpu.VMEM((PACK * ROWS, WINDOW), BF),
            pltpu.VMEM((PACK * ROWS, 256), F32),
        ]
        + extra,
        compiler_params=pltpu.CompilerParams(vmem_limit_bytes=67043328, **talks),
        name="attn_bwd",
    )(length, g, *saved, taps, xt, weight, dres, block, *fulls, *([quarter] if own else []))
MESH = pl.DeviceIdType.MESH
WAYS = ("zh", "zl", "y", "x", "c")
COPIES = 11
STAGES = 6


class Place:
    def __init__(self):
        dp = lax.axis_index("dp")
        self.x = lax.axis_index("tensor")
        self.zh, self.zl = dp // 8, (dp // 4) % 2
        self.y, self.c = (dp // 2) % 2, dp % 2

    def at(self, way):
        spot = {w: getattr(self, w) for w in WAYS}
        spot[way] = 1 - spot[way]
        return {
            "dp": spot["zh"] * 8 + spot["zl"] * 4 + spot["y"] * 2 + spot["c"],
            "tensor": spot["x"],
        }


def greet(place):
    barrier = pltpu.get_barrier_semaphore()
    for way in WAYS:
        pl.semaphore_signal(barrier, inc=1, device_id=place.at(way), device_id_type=MESH)
    pl.semaphore_wait(barrier, len(WAYS))


class Mover:
    def __init__(self, place, send, recv, base):
        self.place, self.send, self.recv, self.base = place, send, recv, base
        self.started = []

    def copy(self, index, src, dst, way):
        return pltpu.make_async_remote_copy(
            src_ref=src, dst_ref=dst,
            send_sem=self.send.at[self.base + index], recv_sem=self.recv.at[self.base + index],
            device_id=self.place.at(way), device_id_type=MESH,
        )

    def push(self, index, src, dst, way):
        copy = self.copy(index, src, dst, way)
        copy.start()
        self.started.append(copy)

    def arrive(self, index, ref, way):
        self.copy(index, ref, ref, way).wait_recv()

    def drain(self):
        for copy in self.started:
            copy.wait_send()


class Gather(Mover):
    def __init__(self, place, shard, whole, lane, width, order, send, recv, base, local, last=4):
        super().__init__(place, send, recv, base)
        self.last = last
        self.shard, self.whole, self.local = shard, whole, local
        self.lane, self.width, self.order = lane, width, order

    def view(self, zh, zl, y, c, x):
        half = self.whole.shape[-1] // 2
        lanes = pl.ds(pl.multiple_of(x * half + self.lane, 128), self.width)
        return self.whole.at[zh, zl, y, c, :, lanes]

    def steps(self, c):
        p, every = self.place, slice(None)
        yield "zh", [self.view(p.zh, p.zl, p.y, c, p.x)], [self.view(1 - p.zh, p.zl, p.y, c, p.x)]
        yield "zl", [self.view(every, p.zl, p.y, c, p.x)], [self.view(every, 1 - p.zl, p.y, c, p.x)]
        if self.order == "yx":
            yield "y", [self.view(every, every, p.y, c, p.x)], [self.view(every, every, 1 - p.y, c, p.x)]
            yield "x", [self.view(every, every, every, c, p.x)], [self.view(every, every, every, c, 1 - p.x)]
        else:
            yield "x", [self.view(every, every, p.y, c, p.x)], [self.view(every, every, p.y, c, 1 - p.x)]
            yield (
                "y",
                [self.view(every, every, p.y, c, x) for x in (0, 1)],
                [self.view(every, every, 1 - p.y, c, x) for x in (0, 1)],
            )

    def run(self, stage):
        p = self.place
        here = self.view(p.zh, p.zl, p.y, p.c, p.x)
        if stage == 0:
            self.mine, self.other = list(self.steps(p.c)), list(self.steps(1 - p.c))
            self.push(0, self.shard, here, "zh")
            self.push(5, self.shard, here, "c")
            self.own = pltpu.make_async_copy(self.shard, here, self.local)
            self.own.start()
        elif stage <= self.last:
            way, _, landed = self.mine[stage - 1]
            for i, ref in enumerate(landed):
                self.arrive(stage - 1 + i, ref, way)
            if stage == 1:
                self.own.wait()
            if stage < self.last:
                way, outgoing, _ = self.mine[stage]
                for i, ref in enumerate(outgoing):
                    self.push(stage + i, ref, ref, way)
            for i, ref in enumerate(landed):
                self.push(5 + stage + i, ref, ref, "c")
        elif stage == self.last + 1:
            self.arrive(5, self.view(p.zh, p.zl, p.y, 1 - p.c, p.x), "c")
            for k in range(self.last):
                for i, ref in enumerate(self.other[k][2]):
                    self.arrive(6 + k + i, ref, "c")
            self.drain()


class GatherEnd(Gather):
    def __init__(self, place, early, whole, lane, width, order, send, recv, base, local):
        Mover.__init__(self, place, send, recv, base)
        self.early, self.whole, self.local = early, whole, local
        self.lane, self.width, self.order = lane, width, order

    def halves_of(self, c):
        p, every = self.place, slice(None)
        if self.order == "yx":
            return "x", [(every, every, every, c, p.x)], [(every, every, every, c, 1 - p.x)]
        return (
            "y",
            [(every, every, p.y, c, x) for x in (0, 1)],
            [(every, every, 1 - p.y, c, x) for x in (0, 1)],
        )

    def old(self, spot):
        now, self.whole = self.whole, self.early
        ref = self.view(*spot)
        self.whole = now
        return ref

    def run(self, stage):
        p, every = self.place, slice(None)
        way, sent, landed = self.halves_of(p.c)
        if stage == 0:
            for i, spot in enumerate(sent):
                self.push(i, self.old(spot), self.view(*spot), way)
            self.loads = []
            if self.order == "yx":
                spots = [(every, every, every, every, p.x)]
            else:
                spots = [(every, every, p.y, every, x) for x in (0, 1)]
            for i, spot in enumerate(spots):
                load = pltpu.make_async_copy(self.old(spot), self.view(*spot), self.local.at[i])
                load.start()
                self.loads.append(load)
        elif stage == 1:
            for i, spot in enumerate(landed):
                self.arrive(i, self.view(*spot), way)
                self.push(2 + i, self.view(*spot), self.view(*spot), "c")
        else:
            for i, spot in enumerate(self.halves_of(1 - p.c)[2]):
                self.arrive(2 + i, self.view(*spot), "c")
            for load in self.loads:
                load.wait()
            self.drain()


class Scatter(Mover):
    def __init__(self, place, full, lane, width, order, out, bufs, send, recv, base, local):
        super().__init__(place, send, recv, base)
        self.full, self.lane, self.width, self.order = full, lane, width, order
        self.out, self.local = out, local
        self.sums, self.in_c, self.in_1, self.in_2, self.in_l, self.in_h = bufs

    def lanes(self, x):
        half = self.full.shape[-1] // 2
        return pl.ds(x * half + self.lane, self.width)

    def add(self, target, landed):
        lead = landed.shape[:-2]
        total = 1
        for n in lead:
            total *= n
        flat_dims = lead

        def one(i, carry):
            index = []
            for n in reversed(flat_dims):
                index.append(i % n)
                i = i // n
            index = tuple(reversed(index))
            target[index] = target[index] + landed[index]
            return carry

        if total == 1:
            one(0, 0)
        else:
            lax.fori_loop(0, total, one, 0)

    def run(self, stage):
        p, every = self.place, slice(None)
        if stage == 0:
            self.loads = []
            for x in (0, 1):
                self.push(x, self.full.at[:, :, :, 1 - p.c, :, self.lanes(x)], self.in_c.at[x], "c")
                load = pltpu.make_async_copy(
                    self.full.at[:, :, :, p.c, :, self.lanes(x)], self.sums.at[x], self.local.at[x]
                )
                load.start()
                self.loads.append(load)
            return
        if stage == 1:
            for x in (0, 1):
                self.arrive(x, self.in_c.at[x], "c")
                self.loads[x].wait()
            self.add(self.sums, self.in_c)
            if self.order == "xy":
                self.push(2, self.sums.at[1 - p.x], self.in_1.at[...], "x")
            else:
                for x in (0, 1):
                    self.push(2 + x, self.sums.at[x, :, :, 1 - p.y], self.in_1.at[x], "y")
        elif stage == 2:
            if self.order == "xy":
                self.arrive(2, self.in_1, "x")
                self.add(self.sums.at[p.x], self.in_1)
                self.push(4, self.sums.at[p.x, :, :, 1 - p.y], self.in_2, "y")
            else:
                for x in (0, 1):
                    self.arrive(2 + x, self.in_1.at[x], "y")
                    self.add(self.sums.at[x, :, :, p.y], self.in_1.at[x])
                self.push(4, self.sums.at[1 - p.x, :, :, p.y], self.in_2, "x")
        elif stage == 3:
            self.arrive(4, self.in_2, "y" if self.order == "xy" else "x")
            self.add(self.sums.at[p.x, :, :, p.y], self.in_2)
            self.push(5, self.sums.at[p.x, :, 1 - p.zl, p.y], self.in_l, "zl")
        elif stage == 4:
            self.arrive(5, self.in_l, "zl")
            self.add(self.sums.at[p.x, :, p.zl, p.y], self.in_l)
            self.push(6, self.sums.at[p.x, 1 - p.zh, p.zl, p.y], self.in_h, "zh")
        else:
            self.arrive(6, self.in_h, "zh")
            self.store(
                self.sums[p.x, p.zh, p.zl, p.y].astype(F32) + self.in_h[...].astype(F32)
            )
            self.drain()

    def store(self, value):
        ref, first = self.out
        ref[:, first : first + self.width] = value


class ScatterStart(Scatter):
    def run(self, stage):
        if stage < 3:
            super().run(stage)
            return
        p = self.place
        self.arrive(4, self.in_2, "y" if self.order == "xy" else "x")
        lanes = slice(self.lane, self.lane + self.width)
        for a in (0, 1):
            for b in (0, 1):
                self.out[a, b, :, lanes] = self.sums[p.x, a, b, p.y] + self.in_2[a, b]
        self.drain()


class ScatterEnd(Mover):
    def __init__(self, place, quarter, out, bufs, send, recv, base):
        super().__init__(place, send, recv, base)
        self.quarter, self.out = quarter, out
        self.in_l, self.sums, self.in_h = bufs

    def run(self, stage):
        p = self.place
        if stage == 0:
            self.push(0, self.quarter.at[:, 1 - p.zl], self.in_l, "zl")
        elif stage == 1:
            self.arrive(0, self.in_l, "zl")
            for a in (0, 1):
                self.sums[a] = self.quarter[a, p.zl] + self.in_l[a]
            self.push(1, self.sums.at[1 - p.zh], self.in_h, "zh")
        else:
            self.arrive(1, self.in_h, "zh")
            self.out[...] = self.sums[p.zh].astype(F32) + self.in_h[...].astype(F32)
            self.drain()


def scatter_scratch(rows, width, order):
    first = (2, 2, 2) if order == "xy" else (2, 2, 2)
    return [
        pltpu.VMEM((2, 2, 2, 2, rows, width), BF),
        pltpu.VMEM((2, 2, 2, 2, rows, width), BF),
        pltpu.VMEM(first + (rows, width), BF),
        pltpu.VMEM((2, 2, rows, width), BF),
        pltpu.VMEM((2, rows, width), BF),
        pltpu.VMEM((rows, width), BF),
    ]


class Total(Mover):
    def __init__(self, place, block, out, sums, landed, send, recv, base, features):
        super().__init__(place, send, recv, base)
        self.features = features
        self.block, self.out, self.sums, self.landed = block, out, sums, landed

    def run(self, stage):
        if stage > 0:
            self.arrive(stage - 1, self.landed.at[stage - 1], WAYS[stage - 1])
            self.sums[stage] = self.sums[stage - 1] + self.landed[stage - 1]
        if stage < 5:
            self.push(stage, self.sums.at[stage], self.landed.at[stage], WAYS[stage])
        else:
            final = self.sums[5]
            self.out[...] = final
            squares = final[STATS : STATS + 1, :]
            self.out[STATS + 1 : STATS + 2, :] = jnp.sqrt(squares / (squares[:, 3:4] * self.features))
            self.drain()


GATHERS = (
    (0, 0, 384, "yx", 0, 0), (0, 384, 384, "xy", 1, 0), (1, 0, 128, "yx", 3, 0),
    (0, 768, 256, "yx", 2, 0), (0, 1024, 128, "xy", 2, 256),
    (3, 0, 384, "yx", 5, 0), (3, 384, 384, "xy", 5, 384),
    (3, 768, 384, "yx", 5, 768), (3, 1152, 384, "xy", 5, 1152),
    (2, 0, 256, "yx", 4, 0), (2, 256, 128, "xy", 4, 256),
    (4, 0, 768, "yx", 6, 0), (4, 768, 768, "xy", 6, 768),
)
GATHER_WAVES = "qqqvvaabbbbdd"
GATHER_LAST = (4,) * 11 + (3, 3)
GATHER_AT = {
    "start": (("q", 0), ("q", 1), ("q", 2), ("v", 0), ("q", 3), ("v", 1), ("a", 0), ("v", 2),
              ("a", 1), ("q", 4), ("b", 0), ("q", 5), ("a", 2)),
    "load": (("v", 3), ("a", 3), ("b", 1), ("d", 0)),
    "newton1": (("v", 4), ("b", 2)),
    "third2": (("v", 5), ("a", 4), ("d", 1)),
    "first1": (("b", 3),),
    "first2": (("a", 5),),
    "mix0": (("d", 2),),
    "end": (("b", 4), ("d", 3), ("b", 5), ("d", 4)),
}
DOWN_GATHERS = GATHERS[-2:]
DOWN_SCATTERS = ((0, 0, 768, "xy"), (0, 768, 768, "yx"))
SCATTERS = (
    (1, 0, 768, "xy", 1, 0), (1, 768, 768, "yx", 1, 768),
    (0, 0, 256, "xy", 0, 0), (0, 256, 128, "yx", 0, 256),
    (2, 768, 256, "xy", 4, 0), (2, 1024, 128, "yx", 4, 256),
    (2, 0, 256, "yx", 2, 0), (2, 256, 128, "xy", 2, 256),
    (2, 384, 256, "xy", 3, 0), (2, 640, 128, "yx", 3, 256),
)
SCATTER_WAVES = "aaaavvqqkk"
SCATTER_AT = {
    "start": (("a", 0), ("d", 0)),
    "second0": (("d", 1), ("a", 1)),
    "second1": (("d", 2),),
    "second2": (("t", 0),),
    "values": (("v", 0), ("t", 1)),
    "newton0": (("t", 2),),
    "newton1": (("t", 3),),
    "newton2": (("a", 2), ("v", 1), ("t", 4)),
    "third1": (("t", 5),),
    "queries": (("q", 0), ("a", 3)),
    "keys": (("k", 0), ("q", 1), ("v", 2)),
    "input0": (("k", 1), ("v", 3), ("q", 2), ("a", 4)),
    "input1": (("k", 2), ("v", 4), ("q", 3), ("k", 3)),
    "end": (("v", 5), ("q", 4), ("k", 4), ("a", 5), ("q", 5), ("k", 5)),
}


def gather_parts(place, cuts, shards, wholes, send, recv, local):
    parts = []
    for n, (i, lane, width, order, source, first) in enumerate(cuts):
        shard = shards[source].at[:, pl.ds(first, width)]
        parts.append(Gather(place, shard, wholes[i], lane, width, order, send, recv, COPIES * n,
                            local.at[n], GATHER_LAST[n]))
    return parts


def gather_scratch(cuts):
    n = len(cuts)
    return [
        pltpu.SemaphoreType.DMA((COPIES * n,)),
        pltpu.SemaphoreType.DMA((COPIES * n,)),
        pltpu.SemaphoreType.DMA((n,)),
    ]


def gather_shapes(rows, wide, units):
    whole = (2, 2, 2, 2)
    return (
        jax.ShapeDtypeStruct(whole + (rows, 3 * wide), BF),
        jax.ShapeDtypeStruct(whole + (BLOCK, 256), F32),
        jax.ShapeDtypeStruct(whole + (rows, wide), BF),
        jax.ShapeDtypeStruct(whole + (rows, units), BF),
        jax.ShapeDtypeStruct(whole + (rows, units), BF),
    )


SUM_COPIES = 7


def scatter_parts(place, cuts, fulls, outs, refs):
    send, recv, local = refs[-3:]
    return [
        Scatter(place, fulls[i], lane, width, order, (outs[n_out], first),
                refs[6 * n : 6 * n + 6], send, recv, SUM_COPIES * n, local.at[n])
        for n, (i, lane, width, order, n_out, first) in enumerate(cuts)
    ]


def all_scatter_scratch(cuts, rows, extra=0):
    out = []
    for _, _, width, order, *_ in cuts:
        out += scatter_scratch(rows, width, order)
    n = len(cuts)
    return out + [
        pltpu.SemaphoreType.DMA((SUM_COPIES * n + extra,)),
        pltpu.SemaphoreType.DMA((SUM_COPIES * n + extra,)),
        pltpu.SemaphoreType.DMA((n, 2)),
    ]


def norm_parts(values):
    centre = values - jnp.mean(values, axis=-1, keepdims=True)
    spread_of = jnp.mean(centre * centre, axis=-1, keepdims=True)
    inverse = lax.rsqrt(spread_of + 1e-05)
    return centre * inverse, inverse


def norm_grad(grad, gain, normal, inverse):
    scaled = grad * gain
    lean = jnp.mean(scaled, axis=-1, keepdims=True)
    along = jnp.mean(scaled * normal, axis=-1, keepdims=True)
    return inverse * (scaled - lean - normal * along)


TURNS = 12


def mid_kernel(slot, wide, *refs):
    (len_ref, ctx_ref, x_ref, cot_ref, outw_ref, inw_ref, partial_ref, gain_ref,
     dctx_ref, res_ref, out_ref, gin_ref, gout_ref, quarter_ref, ends_ref,
     downw_ref, hid_ref, turn_ref, act_ref, slope_ref, acc_ref, dlow_ref, gdown_ref, sum_ref) = refs[:24]
    place = Place()
    greet(place)
    gsend, grecv, glocal = refs[-3 - 3 : -3]
    late = [
        GatherEnd(place, partial_ref, downw_ref, lane, width, order, gsend, grecv, 4 * n, glocal.at[n])
        for n, (_, lane, width, order, *_) in enumerate(DOWN_GATHERS)
    ]
    down = [
        ScatterStart(place, gdown_ref, lane, width, order, quarter_ref,
                     refs[24 + 6 * n : 30 + 6 * n], refs[-3], refs[-2], SUM_COPIES * n, refs[-1].at[n])
        for n, (_, lane, width, order) in enumerate(DOWN_SCATTERS)
    ]

    def both(parts, stage):
        for part in parts:
            part.run(stage)

    both(late, 0)
    hidden_units = act_ref.shape[1]
    step = hidden_units // TURNS
    length = len_ref[lax.axis_index("tensor")]
    gain_one, bias_one = gain_ref[0:1, :], gain_ref[1:2, :]
    gain_two, bias_two = gain_ref[2:3, :], gain_ref[3:4, :]
    sum_ref[...] = jnp.zeros(sum_ref.shape, F32)

    def valid_of(i, rows):
        row = lax.broadcasted_iota(jnp.int32, (rows, 1), 0) + i * rows
        return (row < length).astype(F32)

    def span(i, rows):
        return pl.ds(pl.multiple_of(i * rows, rows), rows)

    def count(row, values):
        sum_ref[row : row + 1, :] += jnp.sum(values, axis=0, keepdims=True)

    def unit(i):
        return pl.ds(pl.multiple_of(i * step, 128), step)

    def weight(ref, lanes):
        return ref[:, :, :, :, :, lanes].reshape(wide, -1)

    def project(i, carry):
        rows = span(i, TALL)
        acc_ref[rows, :] = mm(ctx_ref[rows, :], outw_ref[...], NT)
        return carry

    lax.fori_loop(0, slot // TALL, project, 0)

    def norm_one(i, carry):
        rows = span(i, ROWS)
        valid = valid_of(i, ROWS)
        attn, x = acc_ref[rows, :], x_ref[rows, :].astype(F32)
        count(4, valid * x * x)
        count(5, valid * attn * attn)
        total = x + attn
        res_ref[rows, :] = total
        normal, _ = norm_parts(total)
        hid_ref[rows, :] = (normal * gain_one + bias_one).astype(BF)
        return carry

    lax.fori_loop(0, slot // ROWS, norm_one, 0)

    def expand(i, carry):
        lanes = unit(i)
        for block in range(slot // TALL):
            rows = slice(block * TALL, (block + 1) * TALL)
            pre = mm(hid_ref[rows, :], inw_ref[:, lanes])
            below = 0.5 * (1.0 + lax.erf(pre * 0.5**0.5))
            act_ref[rows, lanes] = (pre * below).astype(BF)
            slope = below + pre * jnp.exp(-0.5 * pre * pre) * (2.0 * jnp.pi) ** -0.5
            slope_ref[rows, lanes] = slope.astype(BF)
        return carry

    lax.fori_loop(0, TURNS, expand, 0)
    both(late, 1)
    both(late, 2)

    def contract(i, carry):
        rows = span(i, 512)
        acc_ref[rows, :] = mm(act_ref[rows, :], weight(downw_ref, slice(None)), NT)
        return carry

    lax.fori_loop(0, slot // 512, contract, 0)

    def norm_two(i, carry):
        rows = span(i, ROWS)
        valid = valid_of(i, ROWS)
        ffn = acc_ref[rows, :]
        count(6, valid * ffn * ffn)
        normal, inverse = norm_parts(hid_ref[rows, :].astype(F32) + ffn)
        out_ref[rows, :] = (normal * gain_two + bias_two).astype(BF)
        grad = cot_ref[rows, :].astype(F32) * valid
        count(2, grad * normal)
        count(3, grad)
        back = norm_grad(grad, gain_two, normal, inverse)
        acc_ref[rows, :] = back
        dlow_ref[rows, :] = back.astype(BF)
        return carry

    lax.fori_loop(0, slot // ROWS, norm_two, 0)
    turn_ref[...] = jnp.transpose(dlow_ref[...])

    def down_grad(i, carry):
        lanes = unit(i)
        value = mm(turn_ref[...], act_ref[:, lanes]).astype(BF)
        gdown_ref[:, :, :, :, :, lanes] = value.reshape(gdown_ref.shape[:-1] + (step,))
        return carry

    lax.fori_loop(0, TURNS, down_grad, 0)
    both(down, 0)
    turn_ref[...] = jnp.transpose(hid_ref[...])

    def back_grad(i, carry):
        lanes = unit(i)
        weights = weight(downw_ref, lanes)
        for block in range(slot // TALL):
            rows = slice(block * TALL, (block + 1) * TALL)
            pre = mm(dlow_ref[rows, :], weights) * slope_ref[rows, lanes].astype(F32)
            slope_ref[rows, lanes] = pre.astype(BF)
        gin_ref[:, lanes] = mm(turn_ref[...], slope_ref[:, lanes]).astype(BF)
        return carry

    lax.fori_loop(0, TURNS // 2, back_grad, 0)
    both(down, 1)
    lax.fori_loop(TURNS // 2, TURNS, back_grad, 0)

    def narrow(i, carry):
        rows = span(i, 512)
        acc_ref[rows, :] += mm(slope_ref[rows, :], inw_ref[...], NT)
        return carry

    lax.fori_loop(0, slot // 512, narrow, 0)
    both(down, 2)

    def norm_one_back(i, carry):
        rows = span(i, ROWS)
        grad = acc_ref[rows, :]
        normal, inverse = norm_parts(res_ref[rows, :])
        count(0, grad * normal)
        count(1, grad)
        back = norm_grad(grad, gain_one, normal, inverse)
        res_ref[rows, :] = back
        dlow_ref[rows, :] = back.astype(BF)
        return carry

    lax.fori_loop(0, slot // ROWS, norm_one_back, 0)
    turn_ref[...] = jnp.transpose(dlow_ref[...])
    for block in range(3):
        rows = slice(block * wide // 3, (block + 1) * wide // 3)
        gout_ref[rows, :] = mm(turn_ref[rows, :], ctx_ref[...]).astype(BF)

    def reach(i, carry):
        rows = span(i, TALL)
        dctx_ref[rows, :] = mm(dlow_ref[rows, :], outw_ref[...]).astype(BF)
        return carry

    lax.fori_loop(0, slot // TALL, reach, 0)
    ends_ref[...] = jnp.zeros(ends_ref.shape, F32)
    tiles = wide // 128
    for n in range(4):
        for tile in range(tiles):
            ends_ref[n * tiles + tile : n * tiles + tile + 1, :] = sum_ref[n : n + 1, tile * 128 : (tile + 1) * 128]
    lane = lax.broadcasted_iota(jnp.int32, (1, 128), 1)
    line = jnp.where(lane == 3, jnp.minimum(length, slot).astype(F32), 0.0)
    for n in range(3):
        line = jnp.where(lane == n, jnp.sum(sum_ref[4 + n : 5 + n, :], axis=1, keepdims=True), line)
    ends_ref[STATS : STATS + 1, :] = line
    both(down, 3)


def mid_call(length, ctx, x, cot, outw, inw, part, gains):
    slot, wide = x.shape
    units = inw.shape[1]
    rows = part.shape[-2]
    shape = jax.ShapeDtypeStruct
    whole = (2, 2, 2, 2, rows, units)
    n = len(DOWN_GATHERS)
    return pl.pallas_call(
        partial(mid_kernel, slot, wide),
        out_shape=(
            shape((slot, wide), BF),
            shape((slot, wide), F32),
            shape((slot, wide), BF),
            shape((wide, units), BF),
            shape((wide, wide), BF),
            shape((2, 2, rows, units // 2), BF),
            shape((40, 128), F32),
        ),
        in_specs=[SM] + [VM] * 5 + [ANY, VM],
        out_specs=[VM] * 7,
        scratch_shapes=[
            pltpu.VMEM(whole, BF),
            pltpu.VMEM((slot, wide), BF),
            pltpu.VMEM((wide, slot), BF),
            pltpu.VMEM((slot, units), BF),
            pltpu.VMEM((slot, units), BF),
            pltpu.VMEM((slot, wide), F32),
            pltpu.VMEM((slot, wide), BF),
            pltpu.VMEM(whole, BF),
            pltpu.VMEM((8, wide), F32),
        ]
        + all_scatter_scratch(DOWN_SCATTERS, rows)[:-3]
        + [
            pltpu.SemaphoreType.DMA((4 * n,)),
            pltpu.SemaphoreType.DMA((4 * n,)),
            pltpu.SemaphoreType.DMA((n, 2)),
        ]
        + all_scatter_scratch(DOWN_SCATTERS, rows)[-3:],
        compiler_params=pltpu.CompilerParams(
            vmem_limit_bytes=67043328, collective_id=4, has_side_effects=True
        ),
        name="middle",
    )(length, ctx, x, cot, outw, inw, part, gains)


D = 768
BOTH = ("tensor", "dp")


def rows_sum(left_op, right_op):
    return lax.dot_general(left_op, right_op, (TN, ((), ())), preferred_element_type=F32)


def cols_sum(left_op, right_op):
    return lax.dot_general(left_op, right_op, (NT, ((), ())), preferred_element_type=F32)


def dense(left_op, right_op):
    return jnp.dot(left_op, right_op, preferred_element_type=F32)


def norm_back(grad, gain, normal, inverse):
    return (
        norm_grad(grad, gain, normal, inverse),
        jnp.sum(grad * normal, axis=0),
        jnp.sum(grad, axis=0),
    )


def gather_plain(pieces):
    sizes = lax.axis_size("tensor"), lax.axis_size("dp")
    out = []
    for piece in pieces:
        joined = lax.all_gather(piece, BOTH, axis=0, tiled=True)
        joined = joined.reshape(sizes[0], sizes[1] * piece.shape[0], piece.shape[1])
        out.append(joined.transpose(1, 0, 2).reshape(joined.shape[1], -1))
    return out


def scatter_plain(fulls):
    parts = lax.axis_size("tensor")
    out = []
    for full in fulls:
        stacked = full.reshape(full.shape[0], parts, -1).transpose(1, 0, 2).reshape(-1, full.shape[1] // parts)
        out.append(lax.psum_scatter(stacked, BOTH, scatter_dimension=0, tiled=True).astype(F32))
    return out


def per_device(own, x_in, lengths, cotangent, w_query, w_key, w_value, w_out, w_in, w_down,
               conv_weight, ln1_gain, ln1_bias, ln2_gain, ln2_bias):
    tensor_index = lax.axis_index("tensor")
    slot = x_in.shape[0]
    parts = lax.axis_size("tensor")
    length = lengths

    later = (w_out.T, w_in, w_down.T)
    few, own_heads, count = ln1_gain.shape[0], conv_weight.shape[0], conv_weight.shape[1]

    def rows_of(array, rows):
        return jnp.pad(array, ((0, rows - array.shape[0]), (0, 128 - array.shape[1])))

    vectors = jnp.stack([ln1_gain, ln1_bias, ln2_gain, ln2_bias])
    block = jnp.concatenate(
        [rows_of(vectors, TAPS_AT), rows_of(conv_weight, FLIP_AT - TAPS_AT),
         rows_of(conv_weight[:, ::-1], BLOCK - FLIP_AT)],
        axis=0,
    )
    if own:
        wholes, saved = attn_fwd(
            length, x_in, parts, own, (w_query, w_key, w_value, block) + later
        )
        qkv_w, blocks, out_w, in_w = (w.reshape(-1, w.shape[-1]) for w in wholes[:4])
        taps = blocks
        blocks = blocks.reshape(lax.axis_size("dp"), BLOCK, parts, 128)
    else:
        qkv_w, out_w, in_w, down_w = gather_plain(
            (jnp.concatenate([w_query, w_key, w_value], axis=1),) + later
        )
        blocks = lax.all_gather(block, ("dp", "tensor"), axis=0)
        blocks = blocks.reshape(-1, parts, BLOCK, 128).transpose(0, 2, 1, 3)
        taps = blocks[0].reshape(BLOCK, parts * 128)
        _, saved = attn_fwd(length, x_in, parts, own, (qkv_w, taps))
    gains = blocks[:, :4, :, :few].transpose(1, 0, 2, 3).reshape(4, D)
    gain_one, bias_one, gain_two, bias_two = gains[0], gains[1], gains[2], gains[3]
    ctx, saved = saved[0], saved[1:]

    if own:
        d_ctx, d_res1, output, grad_in, grad_out, quarter, ends = mid_call(
            length, ctx, x_in, cotangent, out_w, in_w, wholes[4], jnp.pad(gains, ((0, 4), (0, 0)))
        )
        fulls = [grad_out, grad_in]
    else:
        quarter = None
        tokens = x_in.astype(F32)
        mine = lax.dynamic_slice_in_dim(lengths, tensor_index, 1)
        valid = (jnp.arange(slot, dtype=jnp.int32) < mine[0]).astype(F32)[:, None]
        attn_branch = cols_sum(ctx, out_w)
        normal_one, inverse_one = norm_parts(tokens + attn_branch)
        hidden = (normal_one * gain_one + bias_one).astype(BF)
        pre = dense(hidden, in_w)
        below = 0.5 * (1.0 + lax.erf(pre * 0.5**0.5))
        act = (pre * below).astype(BF)
        slope = (below + pre * jnp.exp(-0.5 * pre * pre) * (2.0 * jnp.pi) ** -0.5).astype(BF)
        ffn_branch = cols_sum(act, down_w)
        normal_two, inverse_two = norm_parts(hidden.astype(F32) + ffn_branch)
        output = (normal_two * gain_two + bias_two).astype(BF)
        grad_result = cotangent.astype(F32) * valid
        d_res2, grad_gain_two, grad_bias_two = norm_back(grad_result, gain_two, normal_two, inverse_two)
        d_ffn = d_res2.astype(BF)
        grad_down = rows_sum(d_ffn, act)
        d_pre = (dense(d_ffn, down_w) * slope.astype(F32)).astype(BF)
        grad_in = rows_sum(hidden, d_pre)
        d_hidden = cols_sum(d_pre, in_w) + d_res2
        d_res1, grad_gain_one, grad_bias_one = norm_back(d_hidden, gain_one, normal_one, inverse_one)
        d_attn = d_res1.astype(BF)
        grad_out = rows_sum(d_attn, ctx)
        d_ctx = dense(d_attn, out_w).astype(BF)
        fulls = [grad_out.astype(BF), grad_in.astype(BF), grad_down.astype(BF)]

        def total(branch):
            return jnp.sum(valid * branch * branch)

        sums = jnp.stack([total(tokens), total(attn_branch), total(ffn_branch), jnp.sum(valid)])
        ends = jnp.concatenate(
            [
                jnp.stack([grad_gain_one, grad_bias_one, grad_gain_two, grad_bias_two]).reshape(24, 128),
                jnp.zeros((12, 128), F32),
                jnp.pad(sums[None], ((0, 3), (0, 124))),
            ],
            axis=0,
        )
    grads = attn_bwd(length, d_ctx, saved, taps, x_in.T, qkv_w, d_res1, ends, parts, own, fulls, quarter)
    input_grad, summed = grads[-2:]
    if own:
        weight_grads = (*grads[2:5], grads[0].T, grads[1], grads[5].T)
        stats = summed[STATS + 1, :3]
    else:
        early, (late,) = scatter_plain(fulls), scatter_plain([grads[0]])
        width = late.shape[1] // 3
        weight_grads = (
            late[:, :width], late[:, width : 2 * width], late[:, 2 * width :],
            early[0].T, early[1], early[2].T,
        )
        summed = lax.psum(summed, ("dp", "tensor"))
        stats = jnp.sqrt(summed[STATS, :3] / (summed[STATS, 3] * D))
    share = D // lax.axis_size(("dp", "tensor"))
    start_at = lax.axis_index(("dp", "tensor")) * share
    vectors = lax.dynamic_slice_in_dim(summed[:24].reshape(4, D), start_at, share, 1)
    conv_grad = lax.dynamic_slice_in_dim(summed, 24 + tensor_index * own_heads, own_heads, 0)[:, :count]
    return (
        output, input_grad, *weight_grads,
        conv_grad, vectors[0], vectors[1], vectors[2], vectors[3], stats,
    )


def solution(mesh):
    own = mesh.shape["dp"] == 16 and mesh.shape["tensor"] == 2
    rows, both = P(("dp", "tensor"), None), P(("dp", "tensor"))
    split, crossed = P("dp", "tensor"), P("tensor", "dp")
    return jax.shard_map(
        partial(per_device, own),
        mesh=mesh,
        in_specs=(rows, P("dp"), rows, split, split, split, crossed, split, crossed,
                  P("tensor", None), both, both, both, both),
        out_specs=(rows, rows, split, split, split, crossed, split, crossed,
                   P("tensor", None), both, both, both, both, P()),
        check_vma=False,
    )
```

profile of v0, /device:TPU:0, one launch (start us, length us, event | category | flops | bytes accessed | tf_op | source)
XLA Modules:
  0.0 265.6 jit_solution(10634996204325829765)
XLA Ops:
  0.6 0.8 rev.3
  1.4 0.7 select_maximum_fusion.2
  2.1 1.3 select_maximum_fusion.refs_5_
  3.4 87.0 %attn_fwd.1 = (bf16[2,2,2,2,48,2304]{5,4,3,2,1,0:T(8,128)(2,1)}, f32[2,2,2,2,24,256]{5,4,3,2,1,0:T(8,128)}, bf16[2,2,2,2,48,768]{5,4,3,2,1,0:T(8,128)(2,1)}, bf1...) custom-call(s32[2]{0:T(128)} %refs_0_.5, ...), custom_call_target="tpu_custom_call" | custom-call | tf_op jit(solution)/shard_map/attn_fwd/pallas_call | solution.py:585
  90.4 1.2 reshape_reshape.3
  91.7 0.1 reshape.54
  91.8 0.6 pad.18.refs_7_
  92.4 76.8 %middle.1 = (bf16[1024,768]{1,0:T(8,128)(2,1)}, f32[1024,768]{1,0:T(8,128)}, bf16[1024,768]{1,0:T(8,128)(2,1)}, bf16[768,3072]{1,0:T(8,128)(2,1)}, bf16[768,768]...) custom-call(s32[2]{0:T(128)} %refs_0_.5, bf16[1024,768]{1,0:T(8,128)(2,1)} %get-tuple-element.42.refs_1_, ...), custom_call_target="tpu_custom_call" | custom-call | tf_op jit(solution)/shard_map/middle/pallas_call | solution.py:1274
  169.2 2.6 copy.29
  171.8 82.0 %attn_bwd.1 = (f32[48,384]{1,0:T(8,128)}, f32[48,1536]{1,0:T(8,128)}, f32[48,384]{1,0:T(8,128)}, f32[48,384]{1,0:T(8,128)}, f32[48,384]{1,0:T(8,128)}, /*index=5...) custom-call(s32[2]{0:T(128)} %refs_0_.5, bf16[1024,768]{1,0:T(8,128)(2,1)} %get-tuple-element.48.refs_1_, ...), custom_call_target="tpu_custom_call" | custom-call | tf_op jit(solution)/shard_map/attn_bwd/pallas_call | solution.py:637
  253.8 0.7 slice.26
  254.6 0.1 constant_dynamic-slice_fusion
  254.6 0.5 slice_bitcast_fusion.1
  255.2 1.3 constant_dynamic-slice_fusion.1
  256.5 1.2 slice_bitcast_fusion
  257.6 2.8 %copy.40 = bf16[1024,768]{1,0:T(8,128)(2,1)} copy(bf16[1024,768]{1,0:T(8,128)(2,1)} %get-tuple-element.88) | data formatting | bytes 3145728
  260.5 1.1 copy.41
  261.6 0.0 copy-done.6
  261.6 0.6 copy.42
  262.2 0.6 copy.43
  262.9 0.6 copy.44
  263.5 0.6 copy.45
  264.1 0.7 copy.46
  264.9 0.7 copy.47
  (15 shorter events, 0.1 us)
Async XLA Ops:
  257.6 2.8 %copy-start = (bf16[1024,768]{1,0:T(8,128)(2,1)S(1)}, bf16[1024,768]{1,0:T(8,128)(2,1)}, u32[]{:S(2)}) copy-start(bf16[1024,768]{1,0:T(8,128)(2,1)} %get-tuple-element.89) | copy-start | bytes 4718596
  260.4 1.2 copy-start.6
  260.4 1.8 copy-start.5
  260.4 2.5 copy-start.4
  260.4 3.1 %copy-start.3 = (f32[48,384]{1,0:T(8,128)S(1)}, f32[48,384]{1,0:T(8,128)}, u32[]{:S(2)}) copy-start(f32[48,384]{1,0:T(8,128)} %get-tuple-element.66) | copy-start | bytes 221188
  260.4 3.7 %copy-start.2 = (f32[48,1536]{1,0:T(8,128)S(1)}, f32[48,1536]{1,0:T(8,128)}, u32[]{:S(2)}) copy-start(f32[48,1536]{1,0:T(8,128)} %get-tuple-element.94) | copy-start | bytes 884740
  260.4 4.4 %copy-start.1 = (f32[48,1536]{1,0:T(8,128)S(1)}, f32[48,1536]{1,0:T(8,128)}, u32[]{:S(2)}) copy-start(f32[48,1536]{1,0:T(8,128)} %get-tuple-element.68) | copy-start | bytes 884740
where the time goes:
time: 266 us
  Pallas kernels  246 us (92%)
  local copies, waits for them, and re-layouts  17 us (6%)
    pallas_call x1, Pallas kernels, attn_fwd(): pl.pallas_call(partial(attn_fwd_kernel, slot, groups, parts, own), out_sh...  87 us
    pallas_call x1, Pallas kernels, attn_bwd(): pl.pallas_call(partial(attn_bwd_kernel, slot, groups, parts, own), out_sh...  82 us
    pallas_call x1, Pallas kernels, mid_call(): pl.pallas_call(partial(mid_kernel, slot, wide), out_shape=(shape((slot, w...  76.8 us
    unnamed x23, local copies, waits for them, and re-layouts  10.5 us

commit v1 on v0

--- a/solution.py
+++ b/solution.py
@@ -166,8 +166,17 @@
         weight, taps_ref = outs[0], outs[1].at[0, 0, 0, 0]
     else:
         weight, taps_ref, refs = refs[2], refs[3], refs[4:]
-    ctx_ref, qh_ref, kh_ref, vp_ref, k1_ref, k3_ref, small_ref, chain_ref = refs[:8]
+    ctx_ref, *far, small_ref, far_chain = refs[:8]
     z_ref, k2_ref, s_ref, top_ref, t_ref = refs[8:13]
+    near = refs[13:19]
+    qh_ref, kh_ref, vp_ref, k1_ref, k3_ref, chain_ref = near
+    leave = {
+        name: pltpu.make_async_copy(here, there, refs[19].at[n])
+        for n, (name, here, there) in enumerate(
+            zip(("qh", "kh", "vp", "k1", "k3", "chain"), near, (*far, far_chain))
+        )
+    }
+    refs = refs[:13] + refs[20:]
     moves = []
     if own:
         place = Place()
@@ -216,6 +225,8 @@
         return carry
 
     lax.fori_loop(0, slot // TALL, load, 0)
+    leave["qh"].start()
+    leave["kh"].start()
     advance("load")
     mask = block_mask()
     pmask, one = pair_consts()
@@ -249,6 +260,7 @@
     lax.fori_loop(0, STEPS // 2, newton, 0)
     advance("newton0")
     lax.fori_loop(STEPS // 2, STEPS, newton, 0)
+    leave["chain"].start()
     advance("newton1")
 
     for g in range(groups):
@@ -286,6 +298,7 @@
         lax.fori_loop(0, count, weigh, 0)
         advance(f"third{g}")
 
+    leave["k3"].start()
     ones = mask.astype(F32).astype(BF)
     for g in range(groups):
         at = lanes_of(g)
@@ -300,6 +313,8 @@
 
         lax.fori_loop(0, count, first, 0)
         advance(f"first{g}")
+
+    leave["k1"].start()
 
     def load_values(i, carry):
         rows = pl.ds(pl.multiple_of(i * TALL + EDGE, EDGE), TALL)
@@ -311,6 +326,7 @@
         return carry
 
     lax.fori_loop(0, slot // TALL, load_values, 0)
+    leave["vp"].start()
 
     for g in range(groups):
         at = lanes_of(g)
@@ -336,13 +352,15 @@
         lax.fori_loop(0, count, mix, 0)
         advance(f"mix{g}")
     advance("end")
+    for copy in leave.values():
+        copy.wait()
 
 
 def attn_bwd_kernel(slot, groups, parts, own, *refs):
     (len_ref, g_ref, qh_ref, kh_ref, vp_ref, k1_ref, k3_ref, small_ref, chain_ref, taps_ref,
      xt_ref, w_ref, dres_ref, block_ref) = refs[:14]
     if own:
-        fulls, quarter_ref, refs = refs[14:16], refs[16], refs[17:]
+        fulls, left_refs, refs = refs[14:16], refs[16:18], refs[18:]
         outs, down_out, refs = refs[:5], refs[5], refs[6:]
     else:
         outs, refs = (refs[14],), refs[15:]
@@ -362,10 +380,14 @@
         grad_ref, totals, landed = refs[13:16]
         place = Place()
         greet(place)
-        scatters = scatter_parts(place, SCATTERS, fulls + (grad_ref,), outs, refs[19:])
+        scatters = scatter_parts(place, SCATTERS, fulls + (grad_ref,), outs, refs[26:])
         base = SUM_COPIES * len(SCATTERS)
         total = Total(place, totals.at[0], sum_ref, totals, landed, refs[-3], refs[-2], base, wide_of)
-        tail = ScatterEnd(place, quarter_ref, down_out, refs[16:19], refs[-3], refs[-2], base + 5)
+        tails = [
+            ScatterEnd(place, left_refs[n], down_out, lane, order, refs[16 + 5 * n : 21 + 5 * n],
+                       refs[-3], refs[-2], base + 5 + 3 * n)
+            for n, (_, lane, _, order) in enumerate(DOWN_SCATTERS)
+        ]
         todo = SCATTER_AT
     else:
         grad_ref = outs[0]
@@ -376,7 +398,8 @@
             if which == "t":
                 total.run(stage)
             elif which == "d":
-                tail.run(stage)
+                for tail in tails:
+                    tail.run(stage)
             else:
                 for part, wave in zip(scatters, SCATTER_WAVES):
                     if wave == which:
@@ -596,13 +619,20 @@
             shape((STEPS, KEPT, MARKS, wide), F32),
         ),
         in_specs=[SM, VM] + [VM] * len(weights),
-        out_specs=([VM, VM, ANY, ANY, ANY] if own else []) + [VM] * 8,
+        out_specs=([VM, VM, ANY, ANY, ANY] if own else []) + [VM] + [ANY] * 5 + [VM, ANY],
         scratch_shapes=[
             pltpu.VMEM((2 * groups, 128, 128), F32),
             pltpu.VMEM((2 * groups, 128, 256), BF),
             pltpu.VMEM((slot, WIDE), F32),
             pltpu.VMEM((8, WIDE), F32),
             pltpu.VMEM((PACK * ROWS, WINDOW), BF),
+            pltpu.VMEM((slot, wide), BF),
+            pltpu.VMEM((slot, wide), BF),
+            pltpu.VMEM((slot + 2 * EDGE, wide), BF),
+            pltpu.VMEM((slot, wide), BF),
+            pltpu.VMEM((slot, wide), BF),
+            pltpu.VMEM((STEPS, KEPT, MARKS, wide), F32),
+            pltpu.SemaphoreType.DMA((6,)),
         ]
         + (gather_scratch(GATHERS) if own else []),
         compiler_params=pltpu.CompilerParams(vmem_limit_bytes=LIMIT, **talks),
@@ -611,7 +641,7 @@
     return outs[: len(gathered)], outs[len(gathered) :]
 
 
-def attn_bwd(length, g, saved, taps, xt, weight, dres, block, parts, own, fulls, quarter=None):
+def attn_bwd(length, g, saved, taps, xt, weight, dres, block, parts, own, fulls, left=()):
     slot, wide = g.shape
     groups = wide // WIDE
     shape = jax.ShapeDtypeStruct
@@ -620,24 +650,21 @@
     if own:
         rows = fulls[0].shape[0] // 16
         fulls = [f.reshape(2, 2, 2, 2, rows, f.shape[1]) for f in fulls]
-        width = quarter.shape[-1]
+        width = 2 * left[0].shape[-1]
         outs = (shape((rows, wide // 2), F32), shape((rows, width), F32))
         outs += (shape((rows, wide // 2), F32),) * 3 + (shape((rows, width), F32),)
         extra = [
             pltpu.VMEM((2, 2, 2, 2, rows, 3 * wide), BF),
             pltpu.VMEM((6,) + block.shape, F32),
             pltpu.VMEM((5,) + block.shape, F32),
-            pltpu.VMEM((2, rows, width), BF),
-            pltpu.VMEM((2, rows, width), BF),
-            pltpu.VMEM((rows, width), BF),
-        ] + all_scatter_scratch(SCATTERS, rows, 7)
+        ] + 2 * end_scratch(rows, width // 2) + all_scatter_scratch(SCATTERS, rows, 11)
     else:
         fulls, extra = [], []
         outs = (shape((wide, 3 * wide), BF),)
     return pl.pallas_call(
         partial(attn_bwd_kernel, slot, groups, parts, own),
         out_shape=outs + ends,
-        in_specs=[SM] + [VM] * 7 + [ANY, VM, ANY, ANY, ANY, VM] + [ANY] * len(fulls) + ([VM] if own else []),
+        in_specs=[SM] + [VM] * 7 + [ANY, VM, ANY, ANY, ANY, VM] + [ANY] * len(fulls) + [VM] * len(left),
         out_specs=[VM] * (len(outs) + 2),
         scratch_shapes=[
             pltpu.VMEM(saved[-1].shape, F32),
@@ -660,7 +687,7 @@
         + extra,
         compiler_params=pltpu.CompilerParams(vmem_limit_bytes=67043328, **talks),
         name="attn_bwd",
-    )(length, g, *saved, taps, xt, weight, dres, block, *fulls, *([quarter] if own else []))
+    )(length, g, *saved, taps, xt, weight, dres, block, *fulls, *left)
 MESH = pl.DeviceIdType.MESH
 WAYS = ("zh", "zl", "y", "x", "c")
 COPIES = 11
@@ -906,37 +933,66 @@
 
 class ScatterStart(Scatter):
     def run(self, stage):
-        if stage < 3:
+        if stage < 2:
             super().run(stage)
             return
         p = self.place
-        self.arrive(4, self.in_2, "y" if self.order == "xy" else "x")
-        lanes = slice(self.lane, self.lane + self.width)
-        for a in (0, 1):
-            for b in (0, 1):
-                self.out[a, b, :, lanes] = self.sums[p.x, a, b, p.y] + self.in_2[a, b]
+        for k in (0, 1):
+            if self.order == "xy":
+                if k == 0:
+                    self.arrive(2, self.in_1, "x")
+                here, index = self.sums, lambda a, b, k=k: (p.x, a, b, k)
+                there = lambda a, b, k=k: (a, b, k)
+            else:
+                self.arrive(2 + k, self.in_1.at[k], "y")
+                here, index = self.sums, lambda a, b, k=k: (k, a, b, p.y)
+                there = lambda a, b, k=k: (k, a, b)
+            for a in (0, 1):
+                for b in (0, 1):
+                    self.out[k, a, b] = here[index(a, b)] + self.in_1[there(a, b)]
         self.drain()
 
 
 class ScatterEnd(Mover):
-    def __init__(self, place, quarter, out, bufs, send, recv, base):
+    def __init__(self, place, left, out, lane, order, bufs, send, recv, base):
         super().__init__(place, send, recv, base)
-        self.quarter, self.out = quarter, out
-        self.in_l, self.sums, self.in_h = bufs
+        self.left, self.out, self.lane = left, out, lane
+        self.way = "y" if order == "xy" else "x"
+        self.in_2, self.in_l, self.in_h, self.quarter, self.sums = bufs
 
     def run(self, stage):
         p = self.place
+        mine = getattr(p, self.way)
         if stage == 0:
-            self.push(0, self.quarter.at[:, 1 - p.zl], self.in_l, "zl")
+            self.push(0, self.left.at[1 - mine], self.in_2, self.way)
         elif stage == 1:
-            self.arrive(0, self.in_l, "zl")
+            self.arrive(0, self.in_2, self.way)
+            for a in (0, 1):
+                for b in (0, 1):
+                    self.quarter[a, b] = self.left[mine, a, b] + self.in_2[a, b]
+            self.push(1, self.quarter.at[:, 1 - p.zl], self.in_l, "zl")
+        elif stage == 2:
+            self.arrive(1, self.in_l, "zl")
             for a in (0, 1):
                 self.sums[a] = self.quarter[a, p.zl] + self.in_l[a]
-            self.push(1, self.sums.at[1 - p.zh], self.in_h, "zh")
+            self.push(2, self.sums.at[1 - p.zh], self.in_h, "zh")
         else:
-            self.arrive(1, self.in_h, "zh")
-            self.out[...] = self.sums[p.zh].astype(F32) + self.in_h[...].astype(F32)
+            self.arrive(2, self.in_h, "zh")
+            width = self.in_h.shape[-1]
+            self.out[:, self.lane : self.lane + width] = (
+                self.sums[p.zh].astype(F32) + self.in_h[...].astype(F32)
+            )
             self.drain()
+
+
+def end_scratch(rows, width):
+    return [
+        pltpu.VMEM((2, 2, rows, width), BF),
+        pltpu.VMEM((2, rows, width), BF),
+        pltpu.VMEM((rows, width), BF),
+        pltpu.VMEM((2, 2, rows, width), BF),
+        pltpu.VMEM((2, rows, width), BF),
+    ]
 
 
 def scatter_scratch(rows, width, order):
@@ -1006,7 +1062,7 @@
     "start": (("a", 0), ("d", 0)),
     "second0": (("d", 1), ("a", 1)),
     "second1": (("d", 2),),
-    "second2": (("t", 0),),
+    "second2": (("t", 0), ("d", 3)),
     "values": (("v", 0), ("t", 1)),
     "newton0": (("t", 2),),
     "newton1": (("t", 3),),
@@ -1091,9 +1147,15 @@
 
 
 def mid_kernel(slot, wide, *refs):
-    (len_ref, ctx_ref, x_ref, cot_ref, outw_ref, inw_ref, partial_ref, gain_ref,
-     dctx_ref, res_ref, out_ref, gin_ref, gout_ref, quarter_ref, ends_ref,
-     downw_ref, hid_ref, turn_ref, act_ref, slope_ref, acc_ref, dlow_ref, gdown_ref, sum_ref) = refs[:24]
+    (len_ref, ctx_ref, x_ref, far_cot, outw_ref, far_inw, partial_ref, gain_ref,
+     dctx_ref, res_ref, far_out, far_gin, gout_ref, left_a, left_b, ends_ref,
+     downw_ref, hid_ref, turn_ref, act_ref, slope_ref, acc_ref, dlow_ref, gdown_ref, sum_ref) = refs[:25]
+    cot_ref, inw_ref, out_ref, gin_ref, copies = refs[25:30]
+    get_inw = pltpu.make_async_copy(far_inw, inw_ref, copies.at[0])
+    get_cot = pltpu.make_async_copy(far_cot, cot_ref, copies.at[1])
+    put_out = pltpu.make_async_copy(out_ref, far_out, copies.at[2])
+    put_gin = pltpu.make_async_copy(gin_ref, far_gin, copies.at[3])
+    refs = refs[:24] + refs[30:]
     place = Place()
     greet(place)
     gsend, grecv, glocal = refs[-3 - 3 : -3]
@@ -1102,7 +1164,7 @@
         for n, (_, lane, width, order, *_) in enumerate(DOWN_GATHERS)
     ]
     down = [
-        ScatterStart(place, gdown_ref, lane, width, order, quarter_ref,
+        ScatterStart(place, gdown_ref, lane, width, order, (left_a, left_b)[n],
                      refs[24 + 6 * n : 30 + 6 * n], refs[-3], refs[-2], SUM_COPIES * n, refs[-1].at[n])
         for n, (_, lane, width, order) in enumerate(DOWN_SCATTERS)
     ]
@@ -1112,6 +1174,8 @@
             part.run(stage)
 
     both(late, 0)
+    get_inw.start()
+    get_cot.start()
     hidden_units = act_ref.shape[1]
     step = hidden_units // TURNS
     length = len_ref[lax.axis_index("tensor")]
@@ -1167,6 +1231,7 @@
             slope_ref[rows, lanes] = slope.astype(BF)
         return carry
 
+    get_inw.wait()
     lax.fori_loop(0, TURNS, expand, 0)
     both(late, 1)
     both(late, 2)
@@ -1193,17 +1258,24 @@
         dlow_ref[rows, :] = back.astype(BF)
         return carry
 
+    get_cot.wait()
     lax.fori_loop(0, slot // ROWS, norm_two, 0)
+    put_out.start()
     turn_ref[...] = jnp.transpose(dlow_ref[...])
 
     def down_grad(i, carry):
+        each = TURNS // 4
+        block = i // TURNS
+        i = (i % TURNS) // each * 2 * each + i % each + block * each
         lanes = unit(i)
         value = mm(turn_ref[...], act_ref[:, lanes]).astype(BF)
         gdown_ref[:, :, :, :, :, lanes] = value.reshape(gdown_ref.shape[:-1] + (step,))
         return carry
 
-    lax.fori_loop(0, TURNS, down_grad, 0)
-    both(down, 0)
+    lax.fori_loop(0, TURNS // 2, down_grad, 0)
+    down[0].run(0)
+    lax.fori_loop(TURNS, TURNS + TURNS // 2, down_grad, 0)
+    down[1].run(0)
     turn_ref[...] = jnp.transpose(hid_ref[...])
 
     def back_grad(i, carry):
@@ -1216,9 +1288,12 @@
         gin_ref[:, lanes] = mm(turn_ref[...], slope_ref[:, lanes]).astype(BF)
         return carry
 
-    lax.fori_loop(0, TURNS // 2, back_grad, 0)
-    both(down, 1)
+    lax.fori_loop(0, TURNS // 4, back_grad, 0)
+    down[0].run(1)
+    lax.fori_loop(TURNS // 4, TURNS // 2, back_grad, 0)
+    down[1].run(1)
     lax.fori_loop(TURNS // 2, TURNS, back_grad, 0)
+    put_gin.start()
 
     def narrow(i, carry):
         rows = span(i, 512)
@@ -1226,7 +1301,6 @@
         return carry
 
     lax.fori_loop(0, slot // 512, narrow, 0)
-    both(down, 2)
 
     def norm_one_back(i, carry):
         rows = span(i, ROWS)
@@ -1241,9 +1315,13 @@
 
     lax.fori_loop(0, slot // ROWS, norm_one_back, 0)
     turn_ref[...] = jnp.transpose(dlow_ref[...])
-    for block in range(3):
-        rows = slice(block * wide // 3, (block + 1) * wide // 3)
+
+    def out_grad(i, carry):
+        rows = span(i, TALL)
         gout_ref[rows, :] = mm(turn_ref[rows, :], ctx_ref[...]).astype(BF)
+        return carry
+
+    lax.fori_loop(0, wide // TALL, out_grad, 0)
 
     def reach(i, carry):
         rows = span(i, TALL)
@@ -1261,7 +1339,9 @@
     for n in range(3):
         line = jnp.where(lane == n, jnp.sum(sum_ref[4 + n : 5 + n, :], axis=1, keepdims=True), line)
     ends_ref[STATS : STATS + 1, :] = line
-    both(down, 3)
+    both(down, 2)
+    put_out.wait()
+    put_gin.wait()
 
 
 def mid_call(length, ctx, x, cot, outw, inw, part, gains):
@@ -1279,11 +1359,12 @@
             shape((slot, wide), BF),
             shape((wide, units), BF),
             shape((wide, wide), BF),
-            shape((2, 2, rows, units // 2), BF),
+            shape((2, 2, 2, rows, units // 4), BF),
+            shape((2, 2, 2, rows, units // 4), BF),
             shape((40, 128), F32),
         ),
-        in_specs=[SM] + [VM] * 5 + [ANY, VM],
-        out_specs=[VM] * 7,
+        in_specs=[SM, VM, VM, ANY, VM, ANY, ANY, VM],
+        out_specs=[VM, VM, ANY, ANY, VM, VM, VM, VM],
         scratch_shapes=[
             pltpu.VMEM(whole, BF),
             pltpu.VMEM((slot, wide), BF),
@@ -1294,6 +1375,11 @@
             pltpu.VMEM((slot, wide), BF),
             pltpu.VMEM(whole, BF),
             pltpu.VMEM((8, wide), F32),
+            pltpu.VMEM((slot, wide), BF),
+            pltpu.VMEM(inw.shape, BF),
+            pltpu.VMEM((slot, wide), BF),
+            pltpu.VMEM((wide, units), BF),
+            pltpu.SemaphoreType.DMA((4,)),
         ]
         + all_scatter_scratch(DOWN_SCATTERS, rows)[:-3]
         + [
@@ -1391,12 +1477,12 @@
     ctx, saved = saved[0], saved[1:]
 
     if own:
-        d_ctx, d_res1, output, grad_in, grad_out, quarter, ends = mid_call(
+        d_ctx, d_res1, output, grad_in, grad_out, *left, ends = mid_call(
             length, ctx, x_in, cotangent, out_w, in_w, wholes[4], jnp.pad(gains, ((0, 4), (0, 0)))
         )
         fulls = [grad_out, grad_in]
     else:
-        quarter = None
+        left = ()
         tokens = x_in.astype(F32)
         mine = lax.dynamic_slice_in_dim(lengths, tensor_index, 1)
         valid = (jnp.arange(slot, dtype=jnp.int32) < mine[0]).astype(F32)[:, None]
@@ -1435,7 +1521,7 @@
             ],
             axis=0,
         )
-    grads = attn_bwd(length, d_ctx, saved, taps, x_in.T, qkv_w, d_res1, ends, parts, own, fulls, quarter)
+    grads = attn_bwd(length, d_ctx, saved, taps, x_in.T, qkv_w, d_res1, ends, parts, own, fulls, left)
     input_grad, summed = grads[-2:]
     if own:
         weight_grads = (*grads[2:5], grads[0].T, grads[1], grads[5].T)

time: 266 us -> 256 us (0.962)
  Pallas kernels: 246 us -> 236 us
    pallas_call x1, Pallas kernels: 76.8 us -> 69.3 us  [mid_call(): pl.pallas_call(partial(mid_kernel, slot, wide), out_shape=(shape((slot, w...]
    pallas_call x1, Pallas kernels: 87 us -> 83.2 us  [attn_fwd(): pl.pallas_call(partial(attn_fwd_kernel, slot, groups, parts, own), out_sh...]
where the time goes in v1:
time: 256 us
  Pallas kernels  236 us (92%)
  local copies, waits for them, and re-layouts  17 us (7%)
    pallas_call x1, Pallas kernels, attn_bwd(): pl.pallas_call(partial(attn_bwd_kernel, slot, groups, parts, own), out_sh...  83.7 us
    pallas_call x1, Pallas kernels, attn_fwd(): pl.pallas_call(partial(attn_fwd_kernel, slot, groups, parts, own), out_sh...  83.2 us
    pallas_call x1, Pallas kernels, mid_call(): pl.pallas_call(partial(mid_kernel, slot, wide), out_shape=(shape((slot, w...  69.3 us
    unnamed x23, local copies, waits for them, and re-layouts  10.5 us

profile of v1, /device:TPU:0, one launch (start us, length us, event | category | flops | bytes accessed | tf_op | source)
XLA Modules:
  0.0 256.0 jit_solution(9607263902836051882)
XLA Ops:
  0.6 0.8 rev.3
  1.4 0.7 select_maximum_fusion.2
  2.1 1.3 select_maximum_fusion.refs_5_
  3.4 83.2 %attn_fwd.1 = (bf16[2,2,2,2,48,2304]{5,4,3,2,1,0:T(8,128)(2,1)}, f32[2,2,2,2,24,256]{5,4,3,2,1,0:T(8,128)}, bf16[2,2,2,2,48,768]{5,4,3,2,1,0:T(8,128)(2,1)}, bf1...) custom-call(s32[2]{0:T(128)} %refs_0_.5, ...), custom_call_target="tpu_custom_call" | custom-call | tf_op jit(solution)/shard_map/attn_fwd/pallas_call | solution.py:608
  86.6 1.2 reshape_reshape.3
  87.8 0.1 reshape.54
  88.0 0.6 pad.18.refs_7_
  88.6 69.3 %middle.1 = (bf16[1024,768]{1,0:T(8,128)(2,1)}, f32[1024,768]{1,0:T(8,128)}, bf16[1024,768]{1,0:T(8,128)(2,1)}, bf16[768,3072]{1,0:T(8,128)(2,1)}, bf16[768,768]...) custom-call(s32[2]{0:T(128)} %refs_0_.5, ...), custom_call_target="tpu_custom_call" | custom-call | tf_op jit(solution)/shard_map/middle/pallas_call | solution.py:1354
  157.9 2.6 %copy.29 = bf16[1024,768]{0,1:T(8,128)(2,1)} copy(bf16[1024,768]{1,0:T(8,128)(2,1)} %refs_2_.3) | data formatting | bytes 3145728 | tf_op args[0]
  160.5 83.7 %attn_bwd.1 = (f32[48,384]{1,0:T(8,128)}, f32[48,1536]{1,0:T(8,128)}, f32[48,384]{1,0:T(8,128)}, f32[48,384]{1,0:T(8,128)}, f32[48,384]{1,0:T(8,128)}, /*index=5...) custom-call(s32[2]{0:T(128)} %refs_0_.5, bf16[1024,768]{1,0:T(8,128)(2,1)} %get-tuple-element.49.refs_1_, ...), custom_call_target="tpu_custom_call" | custom-call | tf_op jit(solution)/shard_map/attn_bwd/pallas_call | solution.py:664
  244.3 0.7 slice.26
  245.0 0.1 constant_dynamic-slice_fusion
  245.1 0.5 slice_bitcast_fusion.1
  245.6 1.3 constant_dynamic-slice_fusion.1
  246.9 1.2 slice_bitcast_fusion
  248.1 2.8 %copy.40 = bf16[1024,768]{1,0:T(8,128)(2,1)} copy(bf16[1024,768]{1,0:T(8,128)(2,1)} %get-tuple-element.90) | data formatting | bytes 3145728
  250.9 0.0 copy-start.3
  250.9 1.1 copy.41
  252.1 0.6 copy.42
  252.7 0.6 copy.43
  253.3 0.6 copy.44
  254.0 0.6 copy.45
  254.6 0.7 copy.46
  255.3 0.7 copy.47
  (15 shorter events, 0.1 us)
Async XLA Ops:
  248.1 2.8 %copy-start = (bf16[1024,768]{1,0:T(8,128)(2,1)S(1)}, bf16[1024,768]{1,0:T(8,128)(2,1)}, u32[]{:S(2)}) copy-start(bf16[1024,768]{1,0:T(8,128)(2,1)} %get-tuple-element.91) | copy-start | bytes 4718596
  250.9 1.2 copy-start.6
  250.9 1.8 copy-start.5
  250.9 2.5 copy-start.4
  250.9 3.1 %copy-start.3 = (f32[48,384]{1,0:T(8,128)S(1)}, f32[48,384]{1,0:T(8,128)}, u32[]{:S(2)}) copy-start(f32[48,384]{1,0:T(8,128)} %get-tuple-element.68) | copy-start | bytes 221188
  250.9 3.7 %copy-start.2 = (f32[48,1536]{1,0:T(8,128)S(1)}, f32[48,1536]{1,0:T(8,128)}, u32[]{:S(2)}) copy-start(f32[48,1536]{1,0:T(8,128)} %get-tuple-element.96) | copy-start | bytes 884740
  250.9 4.4 %copy-start.1 = (f32[48,1536]{1,0:T(8,128)S(1)}, f32[48,1536]{1,0:T(8,128)}, u32[]{:S(2)}) copy-start(f32[48,1536]{1,0:T(8,128)} %get-tuple-element.70) | copy-start | bytes 884740

commit v2 on v1

--- a/solution.py
+++ b/solution.py
@@ -368,7 +368,7 @@
     for n, (name, ref) in enumerate(
         (("chain", chain_ref), ("xt", xt_ref), ("w", w_ref), ("dres", dres_ref))
     ):
-        late_ref[name] = pltpu.make_async_copy(ref, refs[2 + n], refs[6].at[n])
+        late_ref[name] = pltpu.make_async_copy(ref, refs[0 if name == "xt" else 2 + n], refs[6].at[n])
     chain_ref, xt_ref, w_ref, dres_ref = refs[2:6]
     dx_ref, sum_ref = refs[:2]
     refs = refs[:2] + refs[7:]
@@ -512,6 +512,7 @@
         lax.fori_loop(0, 4, block_grad, 0)
 
     late_ref["xt"].wait()
+    xt_ref[...] = jnp.transpose(dx_ref[...])
     weight_grad(2 * share, share)
     advance("values")
     late_ref["chain"].wait()
@@ -641,7 +642,7 @@
     return outs[: len(gathered)], outs[len(gathered) :]
 
 
-def attn_bwd(length, g, saved, taps, xt, weight, dres, block, parts, own, fulls, left=()):
+def attn_bwd(length, g, saved, taps, x, weight, dres, block, parts, own, fulls, left=()):
     slot, wide = g.shape
     groups = wide // WIDE
     shape = jax.ShapeDtypeStruct
@@ -668,7 +669,7 @@
         out_specs=[VM] * (len(outs) + 2),
         scratch_shapes=[
             pltpu.VMEM(saved[-1].shape, F32),
-            pltpu.VMEM(xt.shape, BF),
+            pltpu.VMEM((wide, slot), BF),
             pltpu.VMEM(weight.shape, BF),
             pltpu.VMEM(dres.shape, F32),
             pltpu.SemaphoreType.DMA((4,)),
@@ -687,7 +688,7 @@
         + extra,
         compiler_params=pltpu.CompilerParams(vmem_limit_bytes=67043328, **talks),
         name="attn_bwd",
-    )(length, g, *saved, taps, xt, weight, dres, block, *fulls, *left)
+    )(length, g, *saved, taps, x, weight, dres, block, *fulls, *left)
 MESH = pl.DeviceIdType.MESH
 WAYS = ("zh", "zl", "y", "x", "c")
 COPIES = 11
@@ -1232,8 +1233,9 @@
         return carry
 
     get_inw.wait()
-    lax.fori_loop(0, TURNS, expand, 0)
+    lax.fori_loop(0, TURNS * 3 // 4, expand, 0)
     both(late, 1)
+    lax.fori_loop(TURNS * 3 // 4, TURNS, expand, 0)
     both(late, 2)
 
     def contract(i, carry):
@@ -1276,6 +1278,7 @@
     down[0].run(0)
     lax.fori_loop(TURNS, TURNS + TURNS // 2, down_grad, 0)
     down[1].run(0)
+    down[0].run(1)
     turn_ref[...] = jnp.transpose(hid_ref[...])
 
     def back_grad(i, carry):
@@ -1289,10 +1292,8 @@
         return carry
 
     lax.fori_loop(0, TURNS // 4, back_grad, 0)
-    down[0].run(1)
-    lax.fori_loop(TURNS // 4, TURNS // 2, back_grad, 0)
     down[1].run(1)
-    lax.fori_loop(TURNS // 2, TURNS, back_grad, 0)
+    lax.fori_loop(TURNS // 4, TURNS, back_grad, 0)
     put_gin.start()
 
     def narrow(i, carry):
@@ -1521,7 +1522,7 @@
             ],
             axis=0,
         )
-    grads = attn_bwd(length, d_ctx, saved, taps, x_in.T, qkv_w, d_res1, ends, parts, own, fulls, left)
+    grads = attn_bwd(length, d_ctx, saved, taps, x_in, qkv_w, d_res1, ends, parts, own, fulls, left)
     input_grad, summed = grads[-2:]
     if own:
         weight_grads = (*grads[2:5], grads[0].T, grads[1], grads[5].T)

time: 256 us -> 252 us (0.984)
  local copies, waits for them, and re-layouts: 17 us -> 14.4 us
    unnamed x23 -> x22, local copies, waits for them, and re-layouts: 10.5 us -> 7.9 us
where the time goes in v2:
time: 252 us
  Pallas kernels  235 us (93%)
  local copies, waits for them, and re-layouts  14.4 us (6%)
    pallas_call x1, Pallas kernels, attn_fwd(): pl.pallas_call(partial(attn_fwd_kernel, slot, groups, parts, own), out_sh...  83.2 us
    pallas_call x1, Pallas kernels, attn_bwd(): pl.pallas_call(partial(attn_bwd_kernel, slot, groups, parts, own), out_sh...  82.4 us
    pallas_call x1, Pallas kernels, mid_call(): pl.pallas_call(partial(mid_kernel, slot, wide), out_shape=(shape((slot, w...  69 us
    unnamed x22, local copies, waits for them, and re-layouts  7.9 us

profile of v2, /device:TPU:0, one launch (start us, length us, event | category | flops | bytes accessed | tf_op | source)
XLA Modules:
  0.0 251.8 jit_solution(1466930618544227760)
XLA Ops:
  0.6 0.8 rev.3
  1.4 0.7 select_maximum_fusion.2
  2.1 1.3 select_maximum_fusion.refs_5_
  3.4 83.2 %attn_fwd.1 = (bf16[2,2,2,2,48,2304]{5,4,3,2,1,0:T(8,128)(2,1)}, f32[2,2,2,2,24,256]{5,4,3,2,1,0:T(8,128)}, bf16[2,2,2,2,48,768]{5,4,3,2,1,0:T(8,128)(2,1)}, bf1...) custom-call(s32[2]{0:T(128)} %refs_0_.5, ...), custom_call_target="tpu_custom_call" | custom-call | tf_op jit(solution)/shard_map/attn_fwd/pallas_call | solution.py:609
  86.6 1.2 reshape_reshape.3
  87.8 0.1 reshape.54
  88.0 0.6 pad.18.refs_7_
  88.6 69.0 %middle.1 = (bf16[1024,768]{1,0:T(8,128)(2,1)}, f32[1024,768]{1,0:T(8,128)}, bf16[1024,768]{1,0:T(8,128)(2,1)}, bf16[768,3072]{1,0:T(8,128)(2,1)}, bf16[768,768]...) custom-call(s32[2]{0:T(128)} %refs_0_.5, ...), custom_call_target="tpu_custom_call" | custom-call | tf_op jit(solution)/shard_map/middle/pallas_call | solution.py:1355
  157.6 82.4 %attn_bwd.1 = (f32[48,384]{1,0:T(8,128)}, f32[48,1536]{1,0:T(8,128)}, f32[48,384]{1,0:T(8,128)}, f32[48,384]{1,0:T(8,128)}, f32[48,384]{1,0:T(8,128)}, /*index=5...) custom-call(s32[2]{0:T(128)} %refs_0_.5, bf16[1024,768]{1,0:T(8,128)(2,1)} %get-tuple-element.49.refs_1_, ...), custom_call_target="tpu_custom_call" | custom-call | tf_op jit(solution)/shard_map/attn_bwd/pallas_call | solution.py:665
  240.1 0.7 slice.26
  240.8 0.1 constant_dynamic-slice_fusion
  240.9 0.5 slice_bitcast_fusion.1
  241.4 1.3 constant_dynamic-slice_fusion.1
  242.7 1.2 slice_bitcast_fusion
  243.9 2.8 %copy.39 = bf16[1024,768]{1,0:T(8,128)(2,1)} copy(bf16[1024,768]{1,0:T(8,128)(2,1)} %get-tuple-element.90) | data formatting | bytes 3145728
  246.7 1.1 copy.40
  247.8 0.0 copy-done.6
  247.8 0.6 copy.41
  248.5 0.6 copy.42
  249.1 0.0 copy-done.4
  249.1 0.6 copy.43
  249.8 0.6 copy.44
  250.4 0.7 copy.45
  251.1 0.7 copy.46
  (14 shorter events, 0.1 us)
Async XLA Ops:
  243.9 2.8 %copy-start = (bf16[1024,768]{1,0:T(8,128)(2,1)S(1)}, bf16[1024,768]{1,0:T(8,128)(2,1)}, u32[]{:S(2)}) copy-start(bf16[1024,768]{1,0:T(8,128)(2,1)} %get-tuple-element.91) | copy-start | bytes 4718596
  246.7 1.2 copy-start.6
  246.7 1.8 copy-start.5
  246.7 2.5 copy-start.4
  246.7 3.1 %copy-start.3 = (f32[48,384]{1,0:T(8,128)S(1)}, f32[48,384]{1,0:T(8,128)}, u32[]{:S(2)}) copy-start(f32[48,384]{1,0:T(8,128)} %get-tuple-element.68) | copy-start | bytes 221188
  246.7 3.7 %copy-start.2 = (f32[48,1536]{1,0:T(8,128)S(1)}, f32[48,1536]{1,0:T(8,128)}, u32[]{:S(2)}) copy-start(f32[48,1536]{1,0:T(8,128)} %get-tuple-element.96) | copy-start | bytes 884740
  246.7 4.4 %copy-start.1 = (f32[48,1536]{1,0:T(8,128)S(1)}, f32[48,1536]{1,0:T(8,128)}, u32[]{:S(2)}) copy-start(f32[48,1536]{1,0:T(8,128)} %get-tuple-element.70) | copy-start | bytes 884740
